TPU v7x, 32 devices: a whole 2x2x4 slice. The times are simulated.
32 devices in a mesh: iface: 8 (over z, core), sub: 4 (over y, x).
Axes of the slice: x: 2, y: 2, z: 4, core: 2. Of those that a mesh axis runs over, the one named last changes fastest.
Arguments:
- traces: bfloat16 [8, 32, 256, 256], P('iface', 'sub'), may hold values from -6 to 6
- elem_count: int32 [8, 32], P('iface', 'sub'), may hold values from 16 to 64, as said below
- near_idx: int32 [8, 32, 7], P('iface', 'sub'), may hold values from 0 to 31, as said below
- near_count: int32 [8, 32], P('iface', 'sub'), may hold values from 2 to 7, as said below
- near_blocks: bfloat16 [8, 32, 7, 256, 256], P('iface', 'sub'), may hold values from -0.125 to 0.125
- source_map: bfloat16 [8, 32, 128, 256], P('iface', 'sub'), may hold values from -0.125 to 0.125
- m2l_idx: int32 [8, 4, 3], P('iface', 'sub'), may hold values from 0 to 3, as said below
- m2l_count: int32 [8, 4], P('iface', 'sub'), may hold values from 2 to 3, as said below
- translate: bfloat16 [8, 4, 3, 128, 128], P('iface', 'sub'), may hold values from -0.3125 to 0.3125
- evaluate: bfloat16 [8, 32, 256, 128], P('iface', 'sub'), may hold values from -0.5 to 0.5
- send_idx: int32 [8, 4, 2, 4, 16], P('iface', 'sub'), may hold values from 0 to 511
- recv_idx: int32 [8, 4, 2, 4, 16], P('iface', 'sub'), may hold values from 0 to 511
- recv_count: int32 [8, 4, 2, 4], P('iface', 'sub'), may hold values from 0 to 16, as said below
- couple_weight: float32 [8, 4, 2, 4, 16], P('iface', 'sub'), may hold values from 0.25 to 2
Outputs:
- calderon: bfloat16 [8, 32, 256, 256], P('iface', 'sub')
Inputs may be any that keep to these rules, and one draw needn't show every extreme that they name: `near_idx`: each slot names a leaf of the same cluster at most 3 leaves from its own; slot 0 is the leaf 3 before and slot 1 the leaf 3 after, clipped to the cluster. `near_count`: some leaf of every cluster has all slots live. `elem_count`: some leaf of every cluster is full. `m2l_idx`: the slots of a box name every other box of its cluster once each. `m2l_count`: some box of every cluster has all slots live. `recv_count`: for every receiving box and side, one sending box fills all 16 slots.
All inputs are finite; a program needn't handle non-finite values.
Results may differ from a plain program's by a relative error of at most 0.0044.
Values may be sent and summed in bfloat16 or wider, within the bound.
No kernel may reach another device: no remote copies, remote signals or barrier semaphores. Data moves between devices by JAX's collectives and lax.ppermute only.
A program may use at most 64 MiB of HBM per device.

v0:
```python
import jax
import jax.numpy as jnp
from jax import lax
from jax.sharding import PartitionSpec as P

REACH = 3


def with_halo(block, sides, width):
    for axis, dim in sides:
        count = lax.axis_size(axis)
        forward = [(i, i + 1) for i in range(count - 1)]
        backward = [(target, source) for source, target in forward]
        low = lax.ppermute(
            lax.slice_in_dim(block, block.shape[dim] - width, None, axis=dim), axis, forward
        )
        high = lax.ppermute(lax.slice_in_dim(block, 0, width, axis=dim), axis, backward)
        block = jnp.concatenate([low, block, high], axis=dim)
    return block


def shifted(shard, axis, by):
    count = lax.axis_size(axis)
    pairs = [(i, i + by) for i in range(count) if 0 <= i + by < count]
    return lax.ppermute(shard, axis, pairs)


def shards(
    traces,
    elem_count,
    near_idx,
    near_count,
    near_blocks,
    source_map,
    m2l_idx,
    m2l_count,
    translate,
    evaluate,
    send_idx,
    recv_idx,
    recv_count,
    couple_weight,
):
    leaves_here = traces.shape[1]
    row_count = traces.shape[2]
    leaf_size = row_count // 4
    fields = traces.shape[3]
    positions = jnp.arange(leaf_size, dtype=jnp.int32)
    live_leaf = positions[None, :] < elem_count[0][:, None]
    live_rows = jnp.tile(live_leaf, (1, 4))
    masked = jnp.where(live_rows[:, :, None], traces[0], jnp.zeros((), traces.dtype))
    padded = with_halo(masked, (("sub", 0),), REACH)
    my_index = lax.axis_index("sub")
    local_idx = near_idx[0] - my_index * leaves_here + REACH
    picked = padded[local_idx]
    slot_count = near_idx.shape[2]
    slot_live = jnp.arange(slot_count, dtype=jnp.int32)[None, :] < near_count[0][:, None]
    picked = jnp.where(slot_live[:, :, None, None], picked, jnp.zeros((), picked.dtype))
    near_part = jnp.einsum(
        "lsij,lsjn->lin", near_blocks[0], picked, preferred_element_type=jnp.float32
    )
    moment = jnp.einsum(
        "lqj,ljn->qn", source_map[0], masked, preferred_element_type=jnp.float32
    ).astype(jnp.bfloat16)
    wanted = m2l_idx[0, 0]
    trans_slots = wanted.shape[0]
    all_boxes = lax.all_gather(moment[None], "sub", axis=0, tiled=True)
    chosen = all_boxes[wanted]
    m2l_live = jnp.arange(trans_slots, dtype=jnp.int32) < m2l_count[0, 0]
    chosen = jnp.where(m2l_live[:, None, None], chosen, jnp.zeros((), chosen.dtype))
    box_local = jnp.einsum(
        "mpq,mqn->pn", translate[0, 0], chosen, preferred_element_type=jnp.float32
    ).astype(jnp.bfloat16)
    far_part = jnp.einsum("liq,qn->lin", evaluate[0], box_local, preferred_element_type=jnp.float32)
    element_count = leaves_here * leaf_size
    elements = (
        masked.reshape(leaves_here, 4, leaf_size, fields)
        .transpose(0, 2, 1, 3)
        .reshape(element_count, 4, fields)
    )
    outgoing = elements[send_idx[0, 0]]
    owned = lax.all_to_all(outgoing, "sub", split_axis=1, concat_axis=1, tiled=True)
    from_left = shifted(owned[1], "iface", 1)
    from_right = shifted(owned[0], "iface", -1)
    arrived = jnp.stack([from_left, from_right], axis=0)
    slot_total = recv_idx.shape[4]
    slot_valid = (
        jnp.arange(slot_total, dtype=jnp.int32)[None, None, :] < recv_count[0, 0][:, :, None]
    )
    weights = jnp.where(slot_valid, couple_weight[0, 0], jnp.zeros((), jnp.float32))
    sign_row = jnp.array([1.0, 1.0, -1.0, -1.0], dtype=jnp.float32)
    scaled = arrived.astype(jnp.float32) * weights[..., None, None] * sign_row[:, None]
    targets = recv_idx[0, 0].reshape(-1)
    iface_el = (
        jnp.zeros((element_count, 4, fields), jnp.float32)
        .at[targets]
        .add(scaled.reshape(-1, 4, fields))
    )
    iface_part = (
        iface_el.reshape(leaves_here, leaf_size, 4, fields)
        .transpose(0, 2, 1, 3)
        .reshape(leaves_here, row_count, fields)
    )
    total = near_part + far_part + iface_part
    result = jnp.where(live_rows[:, :, None], total, jnp.zeros((), jnp.float32)).astype(
        jnp.bfloat16
    )
    return result[None]


def solution(mesh):
    return jax.shard_map(
        shards,
        mesh=mesh,
        in_specs=(
            P("iface", "sub", None, None),
            P("iface", "sub"),
            P("iface", "sub", None),
            P("iface", "sub"),
            P("iface", "sub", None, None, None),
            P("iface", "sub", None, None),
            P("iface", "sub", None),
            P("iface", "sub"),
            P("iface", "sub", None, None, None),
            P("iface", "sub", None, None),
            P("iface", "sub", None, None, None),
            P("iface", "sub", None, None, None),
            P("iface", "sub", None, None),
            P("iface", "sub", None, None, None),
        ),
        out_specs=P("iface", "sub", None, None),
        check_vma=False,
    )
```

profile of v0, /device:TPU:9, one launch (start us, length us, event | category | flops | bytes accessed | tf_op | source)
XLA Modules:
  0.0 84.7 jit_solution(13542415011376778090)
XLA Ops:
  0.0 0.8 iota_compare_fusion.2
  0.8 0.1 tile.9
  0.9 1.5 %copy.37 = bf16[1,8,256,256]{2,3,1,0:T(8,128)(2,1)S(1)} copy(bf16[1,8,256,256]{3,2,1,0:T(8,128)(2,1)} %param.15) | data formatting | bytes 2097152 | tf_op args[0]
  2.4 0.0 copy-start.1
  2.4 0.1 bitcast_select_fusion
  2.5 0.9 %fusion.38 = (bf16[3,256,256]{1,2,0:T(8,128)(2,1)}, bf16[3,256,256]{1,2,0:T(8,128)(2,1)}) fusion(bf16[8,256,256]{1,2,0:T(8,128)(2,1)S(1)} %bitcast_select_fusion), kind=kLoop, calls=%fused_computation.51 | loop fusion | bytes 1572864 | tf_op jit(solution)/shard_map/slice | solution.py:15
  3.4 3.9 %collective-permute-start = (bf16[3,256,256]{1,2,0:T(8,128)(2,1)}, bf16[3,256,256]{1,2,0:T(8,128)(2,1)}, u32[]{:S(2)}, u32[]{:S(2)}) collective-permute-start(bf16[3,256,256]{1,2,0:T(8,128)(2,1)} %get-tuple-element.5), channel_id=1, source_target_pairs={{0,1},{1,2},{2,3},{4,5},{5,6},{6,7},{8,9},{9,10},{10,11},{12,13},{... | collective-permute-start | bytes 1179656 | tf_op jit(solution)/shard_map/ppermute | solution.py:14
  7.3 1.3 %collective-permute-start.1 = (bf16[3,256,256]{1,2,0:T(8,128)(2,1)}, bf16[3,256,256]{1,2,0:T(8,128)(2,1)}, u32[]{:S(2)}, u32[]{:S(2)}) collective-permute-start(bf16[3,256,256]{1,2,0:T(8,128)(2,1)} %get-tuple-element.6), channel_id=1, source_target_pairs={{1,0},{2,1},{3,2},{5,4},{6,5},{7,6},{9,8},{10,9},{11,10},{13,12},{... | collective-permute-start | bytes 1179656 | tf_op jit(solution)/shard_map/ppermute | solution.py:17
  8.6 0.1 select_bitcast_fusion
  8.7 0.1 copy.41
  8.8 0.0 copy-start.4
  8.9 0.0 copy-start.5
  8.9 0.8 copy.42
  9.7 0.0 copy-start.11
  9.7 0.0 copy-start.7
  9.8 0.1 reshape.218
  9.8 0.8 gather_fusion.2
  10.7 0.0 copy-start.3
  10.7 0.8 copy.43
  11.5 4.3 %all-to-all-start = ((bf16[2,4,16,4,256]{4,3,2,0,1:T(4,128)(2,1)}), bf16[2,4,16,4,256]{4,3,2,0,1:T(4,128)(2,1)S(1)}, u32[]{:S(2)}, u32[]{:S(2)}) async-start(bf16[2,4,16,4,256]{4,3,2,0,1:T(4,128)(2,1)} %copy.43), calls=%async_computation | async-start | bytes 524288 | tf_op jit(solution)/shard_map/all_to_all | solution.py:82
  15.8 0.1 iota_compare_fusion
  15.9 0.1 lt.140
  16.0 0.1 squeeze.47
  16.1 0.1 reshape_squeeze.3
  16.2 0.4 fusion.19
  16.6 15.0 %all-gather = bf16[512,256]{0,1:T(8,128)(2,1)S(1)} all-gather(bf16[128,256]{0,1:T(8,128)(2,1)S(1)} %fusion.19), channel_id=2, replica_groups=mesh['iface'=8,'sub'=4] {'sub'}, dimensions={0}, use_global_device_ids=true | all-gather | bytes 327680 | tf_op jit(solution)/shard_map/all_gather | solution.py:67
  31.6 0.1 copy.51
  32.5 0.1 iota_compare_fusion.1
  32.6 0.0 copy-start.9
  32.6 0.6 gather_fusion.1
  33.2 2.1 %fusion.21 = f32[256,8,256]{2,0,1:T(8,128)} fusion(bf16[1,8,256,128]{3,2,1,0:T(8,128)(2,1)S(1)} %copy-done, bf16[3,128,256]{2,1,0:T(8,128)(2,1)S(1)} %gather_fusion.1, pred[3]{0:T(512)(128)(4,1)S(1)} %iota_compare_fusion.3, bf16[1,1,3,128,128]{4,3,2,1,0:T(8,128)(2,1)S(1)} %copy-done.3), kind=kOutput, calls=%fused_computation.23 | convolution fusion | flops 159514624 | bytes 2916355 | tf_op jit(solution)/shard_map/liq,qn->lin/dot_general | solution.py:74
  35.3 0.1 slice_bitcast_fusion.1
  35.4 4.6 %collective-permute-start.2 = (bf16[4,16,4,256]{3,2,1,0:T(4,128)(2,1)S(1)}, bf16[4,16,4,256]{3,2,1,0:T(4,128)(2,1)S(1)}, u32[]{:S(2)}, u32[]{:S(2)}) collective-permute-start(bf16[4,16,4,256]{3,2,1,0:T(4,128)(2,1)S(1)} %get-tuple-element.7), channel_id=1, source_target_pairs={{0,4},{4,8},{8,12},{12,16},{16,20},{20,24},{24,28},{1,5},{5,9},{9,... | collective-permute-start | bytes 393224 | tf_op jit(solution)/shard_map/ppermute | solution.py:25
  39.9 1.9 %collective-permute-start.3 = (bf16[4,16,4,256]{3,2,1,0:T(4,128)(2,1)S(1)}, bf16[4,16,4,256]{3,2,1,0:T(4,128)(2,1)S(1)}, u32[]{:S(2)}, u32[]{:S(2)}) collective-permute-start(bf16[4,16,4,256]{3,2,1,0:T(4,128)(2,1)S(1)} %get-tuple-element.8), channel_id=1, source_target_pairs={{4,0},{8,4},{12,8},{16,12},{20,16},{24,20},{28,24},{5,1},{9,5},{13... | collective-permute-start | bytes 393224 | tf_op jit(solution)/shard_map/ppermute | solution.py:25
  41.9 0.1 copy.38
  42.0 0.1 reshape.202
  42.1 4.2 %collective-permute-done.3 = bf16[4,16,4,256]{3,2,1,0:T(4,128)(2,1)S(1)} collective-permute-done((bf16[4,16,4,256]{3,2,1,0:T(4,128)(2,1)S(1)}, bf16[4,16,4,256]{3,2,1,0:T(4,128)(2,1)S(1)}, u32[]{:S(2)}, u32[]{:S(2)}) %collective-permute-start.3) | collective-permute-done | bytes 131104 | tf_op jit(solution)/shard_map/ppermute | solution.py:25
  46.2 0.2 pad_maximum_fusion.1
  46.4 0.2 fusion.22
  46.6 1.6 %broadcast_in_dim.80 = f32[512,4,256]{2,1,0:T(4,128)} broadcast(f32[]{:T(128)} %constant.4.clone.1), dimensions={} | broadcast | bytes 2097156 | tf_op jit(solution)/shard_map/broadcast_in_dim | solution.py:95
  48.3 13.6 %scatter_fusion = f32[512,4,256]{2,1,0:T(4,128)} fusion(f32[512,4,256]{2,1,0:T(4,128)} %broadcast_in_dim.80, s32[128]{0:T(128)S(1)} %fusion.34, f32[128,4,256]{2,1,0:T(4,128)S(1)} %fusion.22), kind=kCustom, calls=%fused_computation.3 | custom fusion | flops 131072 | bytes 1573376 | tf_op jit(solution)/shard_map/scatter-add | solution.py:97
  61.9 2.0 %copy.45 = f32[512,4,256]{2,0,1:T(8,128)S(1)} copy(f32[512,4,256]{2,1,0:T(4,128)} %scatter_fusion) | data formatting | bytes 4194304 | tf_op jit(solution)/shard_map/scatter-add | solution.py:97
  63.9 1.5 %copy.46 = f32[8,4,64,256]{3,2,1,0:T(8,128)} copy(f32[8,4,64,256]{3,2,0,1:T(8,128)S(1)} %bitcast.102) | data formatting | bytes 4194304 | tf_op jit(solution)/shard_map/transpose | solution.py:101
  65.4 2.9 %copy.47 = f32[8,256,256]{1,2,0:T(8,128)} copy(f32[8,256,256]{2,1,0:T(8,128)} %bitcast.103) | data formatting | bytes 4194304 | tf_op jit(solution)/shard_map/reshape | solution.py:102
  68.3 1.3 %pad_maximum_fusion = bf16[14,256,256]{1,2,0:T(8,128)(2,1)S(1)} fusion(bf16[3,256,256]{1,2,0:T(8,128)(2,1)} %collective-permute-done.1, bf16[8,256,256]{1,2,0:T(8,128)(2,1)S(1)} %bitcast_select_fusion, bf16[3,256,256]{1,2,0:T(8,128)(2,1)} %collective-permute-done), kind=kLoop, calls=%fused_computation.13 | loop fusion | flops 1835008 | bytes 3670016 | tf_op jit(solution)/shard_map/concatenate | solution.py:18
  69.6 5.3 %gather_fusion = bf16[56,256,256]{1,2,0:T(8,128)(2,1)} fusion(bf16[14,256,256]{1,2,0:T(8,128)(2,1)S(1)} %pad_maximum_fusion, s32[1024]{0:T(1024)S(1)} %pad_clamp_fusion.2), kind=kCustom, calls=%fused_computation | custom fusion | bytes 14680288 | tf_op jit(solution)/shard_map/gather | solution.py:55
  74.9 8.6 %fusion.12 = bf16[1,8,256,256]{2,3,1,0:T(8,128)(2,1)S(1)} fusion(f32[8,256,256]{1,2,0:T(8,128)} %copy.47, f32[256,8,256]{2,0,1:T(8,128)} %fusion.21, bf16[1,8,7,256,256]{4,3,2,1,0:T(8,128)(2,1)} %param.19, bf16[8,7,256,256]{2,3,1,0:T(8,128)(2,1)} %bitcast.104, pred[8,7]{1,0:T(8,128)(4,1)S(1)} %iota_compare_fusion.1, pred[8,256]{1,0:T(8,128)(4,1)S(1)} %tile.9), kind=kOutput, calls=%fused_computation.14 | convolution fusion | flops 1884815360 | bytes 19925048 | tf_op jit(solution)/shard_map/lsij,lsjn->lin/dot_general | solution.py:59
  83.4 1.3 %copy.48 = bf16[1,8,256,256]{3,2,1,0:T(8,128)(2,1)} copy(bf16[1,8,256,256]{2,3,1,0:T(8,128)(2,1)S(1)} %fusion.12) | data formatting | bytes 2097152 | tf_op jit(solution)/shard_map/broadcast_in_dim | solution.py:108
  (31 shorter events, 0.1 us)
Async XLA Ops:
  0.0 33.1 %copy-start = (bf16[1,8,256,128]{3,2,1,0:T(8,128)(2,1)S(1)}, bf16[1,8,256,128]{3,2,1,0:T(8,128)(2,1)}, u32[]{:S(2)}) copy-start(bf16[1,8,256,128]{3,2,1,0:T(8,128)(2,1)} %param.24) | copy-start | bytes 1572868
  2.4 6.2 %copy-start.1 = (bf16[1,8,256,256]{3,2,1,0:T(8,128)(2,1)S(1)}, bf16[1,8,256,256]{3,2,1,0:T(8,128)(2,1)}, u32[]{:S(2)}) copy-start(bf16[1,8,256,256]{3,2,1,0:T(8,128)(2,1)} %param.15) | copy-start | bytes 3145732
  3.4 64.9 %collective-permute-start = (bf16[3,256,256]{1,2,0:T(8,128)(2,1)}, bf16[3,256,256]{1,2,0:T(8,128)(2,1)}, u32[]{:S(2)}, u32[]{:S(2)}) collective-permute-start(bf16[3,256,256]{1,2,0:T(8,128)(2,1)} %get-tuple-element.5), channel_id=1, source_target_pairs={{0,1},{1,2},{2,3},{4,5},{5,6},{6,7},{8,9},{9,10},{10,11},{12,13},{... | collective-permute-start | bytes 1179656 | tf_op jit(solution)/shard_map/ppermute | solution.py:14
  7.3 61.0 %collective-permute-start.1 = (bf16[3,256,256]{1,2,0:T(8,128)(2,1)}, bf16[3,256,256]{1,2,0:T(8,128)(2,1)}, u32[]{:S(2)}, u32[]{:S(2)}) collective-permute-start(bf16[3,256,256]{1,2,0:T(8,128)(2,1)} %get-tuple-element.6), channel_id=1, source_target_pairs={{1,0},{2,1},{3,2},{5,4},{6,5},{7,6},{9,8},{10,9},{11,10},{13,12},{... | collective-permute-start | bytes 1179656 | tf_op jit(solution)/shard_map/ppermute | solution.py:17
  8.7 1.0 %copy-start.6 = (s32[1,1,2,4,16]{4,3,2,1,0:T(4,128)S(1)}, s32[1,1,2,4,16]{4,3,2,1,0:T(4,128)}, u32[]{:S(2)}) copy-start(s32[1,1,2,4,16]{4,3,2,1,0:T(4,128)} %param.25) | copy-start | bytes 1540
  8.8 7.0 %copy-start.8 = (s32[1,1,2,4]{3,2,1,0:T(2,128)S(1)}, s32[1,1,2,4]{3,2,1,0:T(2,128)}, u32[]{:S(2)}) copy-start(s32[1,1,2,4]{3,2,1,0:T(2,128)} %param.27) | copy-start | bytes 100
  8.8 7.1 %copy-start.4 = (f32[1,1,2,4,16]{4,3,2,1,0:T(4,128)S(1)}, f32[1,1,2,4,16]{4,3,2,1,0:T(4,128)}, u32[]{:S(2)}) copy-start(f32[1,1,2,4,16]{4,3,2,1,0:T(4,128)} %param.28) | copy-start | bytes 1540
  8.9 7.2 %copy-start.5 = (s32[1,1,2,4,16]{4,3,2,1,0:T(4,128)S(1)}, s32[1,1,2,4,16]{4,3,2,1,0:T(4,128)}, u32[]{:S(2)}) copy-start(s32[1,1,2,4,16]{4,3,2,1,0:T(4,128)} %param.26) | copy-start | bytes 1540
  8.9 7.3 %copy-start.2 = (bf16[1,8,128,256]{3,2,1,0:T(8,128)(2,1)S(1)}, bf16[1,8,128,256]{3,2,1,0:T(8,128)(2,1)}, u32[]{:S(2)}) copy-start(bf16[1,8,128,256]{3,2,1,0:T(8,128)(2,1)} %param.20) | copy-start | bytes 1572868
  9.7 22.1 %copy-start.10 = (s32[1,1,3]{2,1,0:T(1,128)S(1)}, s32[1,1,3]{2,1,0:T(1,128)}, u32[]{:S(2)}) copy-start(s32[1,1,3]{2,1,0:T(1,128)} %param.21) | copy-start | bytes 40
  9.7 22.8 %copy-start.11 = (s32[1,8]{1,0:T(1,128)S(1)}, s32[1,8]{1,0:T(1,128)}, u32[]{:S(2)}) copy-start(s32[1,8]{1,0:T(1,128)} %param.18) | copy-start | bytes 100
  9.7 22.8 %copy-start.7 = (s32[1,8,7]{1,0,2:T(1,128)S(1)}, s32[1,8,7]{1,0,2:T(1,128)}, u32[]{:S(2)}) copy-start(s32[1,8,7]{1,0,2:T(1,128)} %param.17) | copy-start | bytes 676
  10.7 22.5 %copy-start.3 = (bf16[1,1,3,128,128]{4,3,2,1,0:T(8,128)(2,1)S(1)}, bf16[1,1,3,128,128]{4,3,2,1,0:T(8,128)(2,1)}, u32[]{:S(2)}) copy-start(bf16[1,1,3,128,128]{4,3,2,1,0:T(8,128)(2,1)} %param.23) | copy-start | bytes 294916
  11.5 23.8 %all-to-all-start = ((bf16[2,4,16,4,256]{4,3,2,0,1:T(4,128)(2,1)}), bf16[2,4,16,4,256]{4,3,2,0,1:T(4,128)(2,1)S(1)}, u32[]{:S(2)}, u32[]{:S(2)}) async-start(bf16[2,4,16,4,256]{4,3,2,0,1:T(4,128)(2,1)} %copy.43), calls=%async_computation | async-start | bytes 524288 | tf_op jit(solution)/shard_map/all_to_all | solution.py:82
  32.6 13.9 %copy-start.9 = (f32[4]{0:T(128)S(1)}, f32[4]{0:T(128)}, u32[]{:S(2)}) copy-start(f32[4]{0:T(128)} %constant.6.clone) | copy-start | bytes 52
  35.4 6.7 %collective-permute-start.2 = (bf16[4,16,4,256]{3,2,1,0:T(4,128)(2,1)S(1)}, bf16[4,16,4,256]{3,2,1,0:T(4,128)(2,1)S(1)}, u32[]{:S(2)}, u32[]{:S(2)}) collective-permute-start(bf16[4,16,4,256]{3,2,1,0:T(4,128)(2,1)S(1)} %get-tuple-element.7), channel_id=1, source_target_pairs={{0,4},{4,8},{8,12},{12,16},{16,20},{20,24},{24,28},{1,5},{5,9},{9,... | collective-permute-start | bytes 393224 | tf_op jit(solution)/shard_map/ppermute | solution.py:25
  39.9 6.3 %collective-permute-start.3 = (bf16[4,16,4,256]{3,2,1,0:T(4,128)(2,1)S(1)}, bf16[4,16,4,256]{3,2,1,0:T(4,128)(2,1)S(1)}, u32[]{:S(2)}, u32[]{:S(2)}) collective-permute-start(bf16[4,16,4,256]{3,2,1,0:T(4,128)(2,1)S(1)} %get-tuple-element.8), channel_id=1, source_target_pairs={{4,0},{8,4},{12,8},{16,12},{20,16},{24,20},{28,24},{5,1},{9,5},{13... | collective-permute-start | bytes 393224 | tf_op jit(solution)/shard_map/ppermute | solution.py:25
where the time goes:
time: 86.2 us; the launch traced here: 84.7 us
  local copies, waits for them, and re-layouts  20.9 us (24%)
  other arithmetic  16.6 us (19%)
  starting transfers between devices  16 us (19%)
  blocking collectives  15 us (17%)
  matrix products  11.1 us (13%)
  waiting for transfers between devices  4.18 us (5%)
  between operations  0.98 us (1%)
    all_gather x1, blocking collectives, shards(): all_boxes = lax.all_gather(moment[None], 'sub', axis=0, tiled=True)  15 us
    scatter-add x1, other arithmetic, shards(): iface_el = jnp.zeros((element_count, 4, fields), jnp.float32).at[targets]...  13.6 us
    dot_general x1, matrix products, shards(): jnp.einsum('lsij,lsjn->lin', near_blocks[0], picked, preferred_element_ty...  8.57 us
    ppermute x2, starting transfers between devices, shifted(): return lax.ppermute(shard, axis, pairs)  6.51 us
    gather x1, local copies, waits for them, and re-layouts, shards(): picked = padded[local_idx]  5.26 us
    all_to_all x1, starting transfers between devices, shards(): lax.all_to_all(outgoing, 'sub', split_axis=1, concat_axis=1, tiled=True)  4.32 us
    ppermute x2, waiting for transfers between devices, shifted(): return lax.ppermute(shard, axis, pairs)  4.17 us
    ppermute x1, starting transfers between devices, with_halo(): lax.ppermute(lax.slice_in_dim(block, block.shape[dim] - width, None, axis...  3.86 us
  transfers between devices with their start and end apart: 5, of which 1 were waited for; matrix products, arithmetic and copies ran while one was open for 34% of the time, Pallas kernels for 0%

commit v1 on v0

v1 whole, which is shorter than its diff:
```python
import functools

import jax
import jax.numpy as jnp
from jax import lax
from jax.experimental import pallas as pl
from jax.experimental.pallas import tpu as pltpu
from jax.sharding import PartitionSpec as P

REACH = 3
MIB = 1 << 20
F32 = jnp.float32
BF16 = jnp.bfloat16


def dot(a, b):
    return jnp.dot(a, b, preferred_element_type=F32)


def live_rows(count, leaf_size, rows, fields):
    row = lax.broadcasted_iota(jnp.int32, (rows, fields), 0)
    return lax.rem(row, leaf_size) < count


def pack_kernel(sides, owners, slots, count_ref, send_ref, x_ref, source_ref, out_ref, xm_ref):
    leaves, rows, fields = x_ref.shape
    leaf_size = rows // 4
    moment = jnp.zeros((source_ref.shape[1], fields), F32)
    picks = []
    send = send_ref[...]
    total = sides * owners * slots
    for l in range(leaves):
        live = live_rows(count_ref[0, l], leaf_size, rows, fields)
        x = jnp.where(live, x_ref[l].astype(F32), 0.0).astype(BF16)
        xm_ref[l] = x
        moment += dot(source_ref[l], x)
        element = lax.broadcasted_iota(jnp.int32, (total, leaf_size), 1) + l * leaf_size
        picks.append(jnp.where(element == send, 1.0, 0.0).astype(BF16))
    pick = jnp.concatenate(picks, axis=1)
    for c in range(4):
        comp = xm_ref[:, c * leaf_size : (c + 1) * leaf_size, :]
        got = dot(pick, comp.reshape(leaves * leaf_size, fields)).astype(BF16)
        for s in range(sides):
            for o in range(owners):
                at = (s * owners + o) * slots
                base = (s * 4 + c) * slots
                out_ref[o, base : base + slots, :] = got[at : at + slots]
    moment = moment.astype(BF16)
    for o in range(owners):
        out_ref[o, sides * 4 * slots :, :] = moment


def apply_kernel(
    boxes,
    slots,
    count_ref,
    table_ref,
    m2l_ref,
    m2l_count_ref,
    recv_ref,
    weight_ref,
    x_ref,
    near_ref,
    first_ref,
    second_ref,
    moment_ref,
    translate_ref,
    evaluate_ref,
    left_ref,
    right_ref,
    out_ref,
    src_ref,
    part_ref,
):
    leaves, rows, fields = x_ref.shape
    leaf_size = rows // 4
    near_slots = near_ref.shape[1]
    for l in range(leaves):
        live = live_rows(count_ref[0, l], leaf_size, rows, fields)
        src_ref[l] = jnp.where(live, x_ref[l].astype(F32), 0.0).astype(BF16)
    for i in range(REACH):
        src_ref[leaves + i] = first_ref[i]
        src_ref[leaves + REACH + i] = second_ref[i]
    src_ref[leaves + 2 * REACH] = jnp.zeros((rows, fields), BF16)

    local = jnp.zeros((translate_ref.shape[1], fields), F32)
    q = moment_ref.shape[1] - 8 * slots
    for t in range(translate_ref.shape[0]):
        moment = moment_ref[m2l_ref[0, t], 8 * slots :, :]
        moment = jnp.where(t < m2l_count_ref[0, 0], moment.astype(F32), 0.0).astype(BF16)
        local += dot(translate_ref[t], moment)
    local = local.astype(BF16)

    slot_total = recv_ref.shape[1]
    weight = weight_ref[...]
    high = weight.astype(BF16).astype(F32)
    low = weight - high
    element = lax.broadcasted_iota(jnp.int32, (leaves * leaf_size, slot_total), 0)
    hit = element == recv_ref[...]
    spread = jnp.concatenate(
        [jnp.where(hit, high, 0.0).astype(BF16), jnp.where(hit, low, 0.0).astype(BF16)], axis=1
    )
    for c in range(4):
        comp = [
            ref[:, c * slots : (c + 1) * slots, :].reshape(boxes * slots, fields)
            for ref in (left_ref, right_ref)
        ]
        arrived = jnp.concatenate(comp + comp, axis=0)
        part = dot(spread, arrived)
        part = part if c < 2 else -part
        part_ref[:, c * leaf_size : (c + 1) * leaf_size, :] = part.reshape(
            leaves, leaf_size, fields
        )

    def one_leaf(l, carry):
        total = dot(evaluate_ref[l], local) + part_ref[l]
        for s in range(near_slots):
            total += dot(near_ref[l, s], src_ref[table_ref[l, s]])
        live = live_rows(count_ref[0, l], leaf_size, rows, fields)
        out_ref[l] = jnp.where(live, total, 0.0).astype(BF16)
        return carry

    lax.fori_loop(0, leaves, one_leaf, 0)


def smem():
    return pl.BlockSpec(memory_space=pltpu.SMEM)


def vmem():
    return pl.BlockSpec(memory_space=pltpu.VMEM)


def shards(
    traces,
    elem_count,
    near_idx,
    near_count,
    near_blocks,
    source_map,
    m2l_idx,
    m2l_count,
    translate,
    evaluate,
    send_idx,
    recv_idx,
    recv_count,
    couple_weight,
):
    x = traces[0]
    leaves, rows, fields = x.shape
    leaf_size = rows // 4
    q = source_map.shape[2]
    sides, owners, slots = send_idx.shape[2:]
    near_slots = near_idx.shape[2]
    groups = lax.axis_size("iface")
    boxes = lax.axis_size("sub")
    me = lax.axis_index("sub")
    odd = lax.rem(me, 2)

    def edge(start):
        piece = lax.dynamic_slice_in_dim(x, start, REACH, 0)
        count = lax.dynamic_slice_in_dim(elem_count[0], start, REACH, 0)
        row = lax.broadcasted_iota(jnp.int32, (REACH, rows, fields), 1)
        return jnp.where(row % leaf_size < count[:, None, None], piece, jnp.zeros((), BF16))

    last = leaves - REACH
    pairs = [(b, b ^ 1) for b in range(boxes) if b ^ 1 < boxes]
    first = lax.ppermute(edge(jnp.where(odd == 0, last, 0)), "sub", pairs)
    up = [(b, b + 1) for b in range(1, boxes - 1, 2)]
    second = lax.ppermute(
        edge(jnp.where(odd == 0, 0, last)), "sub", up + [(j, i) for i, j in up]
    )

    chunk_rows = sides * 4 * slots
    chunks = pl.pallas_call(
        functools.partial(pack_kernel, sides, owners, slots),
        out_shape=jax.ShapeDtypeStruct((owners, chunk_rows + q, fields), BF16),
        in_specs=[smem(), vmem(), vmem(), vmem()],
        out_specs=vmem(),
        scratch_shapes=[pltpu.VMEM((leaves, rows, fields), BF16)],
        compiler_params=pltpu.CompilerParams(vmem_limit_bytes=24 * MIB),
        cost_estimate=pl.CostEstimate(flops=3 * 10**8, bytes_accessed=2 * MIB, transcendentals=0),
        name="pack",
    )(elem_count, send_idx.reshape(-1, 1), x, source_map[0])
    owned = lax.all_to_all(chunks, "sub", split_axis=0, concat_axis=0, tiled=True)
    half = chunk_rows // 2
    left = lax.ppermute(owned[:, half:chunk_rows], "iface", [(g, g + 1) for g in range(groups - 1)])
    right = lax.ppermute(owned[:, :half], "iface", [(g + 1, g) for g in range(groups - 1)])

    near = near_idx[0] - me * leaves
    low = jnp.where(odd == 0, leaves + REACH, leaves)
    high = jnp.where(odd == 0, leaves, leaves + REACH)
    table = jnp.where(near < 0, near + REACH + low, jnp.where(near < leaves, near, near - leaves + high))
    slot_at = lax.broadcasted_iota(jnp.int32, (leaves, near_slots), 1)
    table = jnp.where(slot_at < near_count[0][:, None], table, leaves + 2 * REACH)
    valid = lax.broadcasted_iota(jnp.int32, (sides, boxes, slots), 2) < recv_count[0, 0][:, :, None]
    weight = jnp.where(valid, couple_weight[0, 0], jnp.zeros((), F32)).reshape(1, -1)

    out = pl.pallas_call(
        functools.partial(apply_kernel, boxes, slots),
        out_shape=jax.ShapeDtypeStruct((leaves, rows, fields), BF16),
        in_specs=[smem(), smem(), smem(), smem()] + [vmem()] * 11,
        out_specs=vmem(),
        scratch_shapes=[
            pltpu.VMEM((leaves + 2 * REACH + 1, rows, fields), BF16),
            pltpu.VMEM((leaves, rows, fields), F32),
        ],
        compiler_params=pltpu.CompilerParams(vmem_limit_bytes=48 * MIB),
        cost_estimate=pl.CostEstimate(flops=24 * 10**8, bytes_accessed=12 * MIB, transcendentals=0),
        name="apply",
    )(
        elem_count,
        table,
        m2l_idx[0],
        m2l_count,
        recv_idx.reshape(1, -1),
        weight,
        x,
        near_blocks[0],
        first,
        second,
        owned,
        translate[0, 0],
        evaluate[0],
        left,
        right,
    )
    return out[None]


def solution(mesh):
    def split(rank):
        return P("iface", "sub", *(None,) * (rank - 2))

    return jax.shard_map(
        shards,
        mesh=mesh,
        in_specs=tuple(split(rank) for rank in (4, 2, 3, 2, 5, 4, 3, 2, 5, 4, 5, 5, 4, 5)),
        out_specs=split(4),
        check_vma=False,
    )
```

time: 86.2 us -> 48.9 us (0.57)
  the two profiles are of different devices: /device:TPU:9 before, /device:TPU:0 now
where the time goes in v1:
time: 48.9 us; the launch traced here: 48.2 us
  starting transfers between devices  14.9 us (30%)
  local copies, waits for them, and re-layouts  11.4 us (23%)
  Pallas kernels  10 us (20%)
  waiting for transfers between devices  8.32 us (17%)
  other arithmetic  2.84 us (6%)
  between operations  0.74 us (2%)
    ppermute x1, waiting for transfers between devices, shards(): first = lax.ppermute(edge(jnp.where(odd == 0, last, 0)), 'sub', pairs)  8.31 us
    pallas_call x1, Pallas kernels, shards(): pl.pallas_call(functools.partial(apply_kernel, boxes, slots), out_shape=j...  8.16 us
    unnamed x17, local copies, waits for them, and re-layouts  8.15 us
    all_to_all x1, starting transfers between devices, shards(): lax.all_to_all(chunks, 'sub', split_axis=0, concat_axis=0, tiled=True)  5.16 us
    ppermute x1, starting transfers between devices, shards(): first = lax.ppermute(edge(jnp.where(odd == 0, last, 0)), 'sub', pairs)  4.77 us
    ppermute x1, starting transfers between devices, shards(): lax.ppermute(owned[:, half:chunk_rows], 'iface', [(g, g + 1) for g in ran...  3.04 us
    pallas_call x1, Pallas kernels, shards(): pl.pallas_call(functools.partial(pack_kernel, sides, owners, slots), out_...  1.87 us
    select_n x1, other arithmetic, edge(): jnp.where(row % leaf_size < count[:, None, None], piece, jnp.zeros((), BF...  1.35 us
  transfers between devices with their start and end apart: 5, of which 1 were waited for; matrix products, arithmetic and copies ran while one was open for 13% of the time, Pallas kernels for 0%

profile of v1, /device:TPU:0, one launch (start us, length us, event | category | flops | bytes accessed | tf_op | source)
XLA Modules:
  0.0 48.2 jit_solution(18001268481520982908)
XLA Ops:
  0.0 0.8 %reshape.53.send_ref = s32[128,1]{1,0:T(8,128)S(1)} reshape(s32[1,1,2,4,16]{4,3,2,1,0:T(4,128)} %param.24) | data formatting | bytes 1024 | tf_op jit(solution)/shard_map/reshape | solution.py:185
  0.8 0.0 copy-start
  0.8 1.2 %copy-done = bf16[1,8,256,256]{3,2,1,0:T(8,128)(2,1)S(1)} copy-done((bf16[1,8,256,256]{3,2,1,0:T(8,128)(2,1)S(1)}, bf16[1,8,256,256]{3,2,1,0:T(8,128)(2,1)}, u32[]{:S(2)}) %copy-start) | copy-done | bytes 1048600
  2.0 0.0 copy-start.2
  2.0 1.0 %copy-done.2 = bf16[1,8,128,256]{3,2,1,0:T(8,128)(2,1)S(1)} copy-done((bf16[1,8,128,256]{3,2,1,0:T(8,128)(2,1)S(1)}, bf16[1,8,128,256]{3,2,1,0:T(8,128)(2,1)}, u32[]{:S(2)}) %copy-start.2) | copy-done | bytes 524312
  3.0 0.0 copy-start.5
  3.1 0.7 %copy-done.5 = s32[1,8]{1,0:T(1,128)S(1)} copy-done((s32[1,8]{1,0:T(1,128)S(1)}, s32[1,8]{1,0:T(1,128)}, u32[]{:S(2)}) %copy-start.5) | copy-done | bytes 56
  3.7 1.9 %pack.1 = bf16[4,256,256]{2,1,0:T(8,128)(2,1)} custom-call(s32[1,8]{1,0:T(1,128)S(1)} %copy-done.5, s32[128,1]{1,0:T(8,128)S(1)} %reshape.53.send_ref, bf16[8,256,256]{2,1,0:T(8,128)(2,1)S(1)} %bitcast.32, bf16[8,128,256]{2,1,0:T(8,128)(2,1)S(1)} %bitcast.34), custom_call_target="tpu_custom_call" | custom-call | flops 300000000 | bytes 2097152 | tf_op jit(solution)/shard_map/pack/pallas_call | solution.py:176
  5.6 5.2 %all-to-all-start = ((bf16[4,256,256]{2,1,0:T(8,128)(2,1)}), bf16[4,256,256]{2,1,0:T(8,128)(2,1)S(1)}, u32[]{:S(2)}, u32[]{:S(2)}) async-start(bf16[4,256,256]{2,1,0:T(8,128)(2,1)} %pack.1), calls=%async_computation | async-start | bytes 1048576 | tf_op jit(solution)/shard_map/all_to_all | solution.py:186
  10.7 0.8 %fusion.8 = (s32[3]{0:T(128)S(1)}, s32[3]{0:T(128)S(1)}) fusion(s32[1,8]{1,0:T(1,128)} %count_ref.3, s32[]{:T(128)S(6)} %select_n.66, s32[]{:T(128)S(6)} %select_n.64), kind=kLoop, calls=%fused_computation.20 | loop fusion | bytes 56 | tf_op jit(solution)/shard_map/lt | solution.py:165
  11.6 1.3 %fusion.1 = (bf16[3,256,256]{2,1,0:T(8,128)(2,1)S(1)}, bf16[3,256,256]{2,1,0:T(8,128)(2,1)S(1)}) fusion(bf16[1,8,256,256]{3,2,1,0:T(8,128)(2,1)} %param.14, s32[]{:T(128)S(6)} %select_n.66, s32[3]{0:T(128)S(1)} %get-tuple-element.9, s32[256]{0:T(256)S(1)} %get-tuple-element.11, s32[256]{0:T(256)S(1)} %get-tuple-element.12, ...), kind=kLoop, calls=%fused_computation.3 | loop fusion | flops 983040 | bytes 1575200 | tf_op jit(solution)/shard_map/jit(_where)/select_n | solution.py:165
  12.9 0.7 %collective-permute-start.1 = (bf16[3,256,256]{2,1,0:T(8,128)(2,1)S(1)}, bf16[3,256,256]{2,1,0:T(8,128)(2,1)S(1)}, u32[]{:S(2)}, u32[]{:S(2)}) collective-permute-start(bf16[3,256,256]{2,1,0:T(8,128)(2,1)S(1)} %get-tuple-element.5), channel_id=1, source_target_pairs={{1,2},{2,1},{5,6},{6,5},{9,10},{10,9},{13,14},{14,13},{17,18},{18,... | collective-permute-start | bytes 1179656 | tf_op jit(solution)/shard_map/ppermute | solution.py:171
  13.6 4.8 %collective-permute-start = (bf16[3,256,256]{2,1,0:T(8,128)(2,1)S(1)}, bf16[3,256,256]{2,1,0:T(8,128)(2,1)S(1)}, u32[]{:S(2)}, u32[]{:S(2)}) collective-permute-start(bf16[3,256,256]{2,1,0:T(8,128)(2,1)S(1)} %get-tuple-element.6), channel_id=1, source_target_pairs={{0,1},{1,0},{2,3},{3,2},{4,5},{5,4},{6,7},{7,6},{8,9},{9,8},{10,11... | collective-permute-start | bytes 1179656 | tf_op jit(solution)/shard_map/ppermute | solution.py:169
  19.0 0.8 %reshape.51.recv_ref = s32[1,128]{1,0:T(1,128)S(1)} reshape(s32[1,1,2,4,16]{4,3,2,1,0:T(4,128)} %param.25) | data formatting | bytes 1024 | tf_op jit(solution)/shard_map/reshape | solution.py:217
  19.8 0.8 %squeeze.25 = f32[1,128]{1,0:T(1,128)S(1)} reshape(f32[1,1,2,4,16]{4,3,2,1,0:T(4,128)} %param.27) | data formatting | bytes 1024 | tf_op jit(solution)/shard_map/squeeze | solution.py:198
  20.6 0.8 %iota_compare_fusion = pred[2,4,16]{2,1,0:T(4,128)(4,1)S(1)} fusion(s32[2,4]{1,0:T(2,128)} %bitcast.39), kind=kLoop, calls=%fused_computation.12 | loop fusion | flops 128 | bytes 160 | tf_op jit(solution)/shard_map/lt | solution.py:197
  21.3 0.1 lt.82
  21.4 0.8 %copy.15 = s32[1,8,7]{2,1,0:T(8,128)S(1)} copy(s32[1,8,7]{1,0,2:T(1,128)} %param.16) | data formatting | bytes 448 | tf_op args[2]
  22.2 0.7 %fusion.3.table_ref = s32[8,7]{1,0:T(8,128)S(1)} fusion(s32[1,8,7]{2,1,0:T(8,128)S(1)} %copy.15, s32[]{:T(128)S(6)} %select_n.58, s32[]{:T(128)S(6)} %select_n.57, s32[]{:T(128)S(6)} %mul.3, s32[8]{0:T(128)} %bitcast.40), kind=kLoop, calls=%fused_computation.6 | loop fusion | flops 616 | bytes 492 | tf_op jit(solution)/shard_map/jit(_where)/select_n | solution.py:196
  22.9 0.0 all-to-all-done.moment_ref
  22.9 1.3 %collective-permute-start.3 = (bf16[4,64,256]{2,1,0:T(8,128)(2,1)S(1)}, bf16[4,64,256]{2,1,0:T(8,128)(2,1)S(1)}, u32[]{:S(2)}, u32[]{:S(2)}) collective-permute-start(bf16[4,64,256]{2,1,0:T(8,128)(2,1)S(1)} %get-tuple-element.7), channel_id=1, source_target_pairs={{4,0},{8,4},{12,8},{16,12},{20,16},{24,20},{28,24},{5,1},{9,5},{13... | collective-permute-start | bytes 393224 | tf_op jit(solution)/shard_map/ppermute | solution.py:189
  24.2 3.0 %collective-permute-start.2 = (bf16[4,64,256]{2,1,0:T(8,128)(2,1)S(1)}, bf16[4,64,256]{2,1,0:T(8,128)(2,1)S(1)}, u32[]{:S(2)}, u32[]{:S(2)}) collective-permute-start(bf16[4,64,256]{2,1,0:T(8,128)(2,1)S(1)} %get-tuple-element.8), channel_id=1, source_target_pairs={{0,4},{4,8},{8,12},{12,16},{16,20},{20,24},{24,28},{1,5},{5,9},{9,... | collective-permute-start | bytes 393224 | tf_op jit(solution)/shard_map/ppermute | solution.py:188
  27.3 0.0 collective-permute-done.1.second_ref
  27.3 8.3 %collective-permute-done.first_ref = bf16[3,256,256]{2,1,0:T(8,128)(2,1)S(1)} collective-permute-done((bf16[3,256,256]{2,1,0:T(8,128)(2,1)S(1)}, bf16[3,256,256]{2,1,0:T(8,128)(2,1)S(1)}, u32[]{:S(2)}, u32[]{:S(2)}) %collective-permute-start) | collective-permute-done | bytes 393248 | tf_op jit(solution)/shard_map/ppermute | solution.py:169
  35.6 0.0 collective-permute-done.3.right_ref
  35.6 0.0 collective-permute-done.2.left_ref
  35.6 0.0 copy-start.1
  35.6 1.2 %copy-done.1 = bf16[1,8,256,256]{3,2,1,0:T(8,128)(2,1)S(1)} copy-done((bf16[1,8,256,256]{3,2,1,0:T(8,128)(2,1)S(1)}, bf16[1,8,256,256]{3,2,1,0:T(8,128)(2,1)}, u32[]{:S(2)}) %copy-start.1) | copy-done | bytes 1048600
  36.8 0.0 copy-start.3
  36.8 1.0 %copy-done.3 = bf16[1,8,256,128]{3,2,1,0:T(8,128)(2,1)S(1)} copy-done((bf16[1,8,256,128]{3,2,1,0:T(8,128)(2,1)S(1)}, bf16[1,8,256,128]{3,2,1,0:T(8,128)(2,1)}, u32[]{:S(2)}) %copy-start.3) | copy-done | bytes 524312
  37.9 0.0 copy-start.4
  37.9 0.9 %copy-done.4 = bf16[1,1,3,128,128]{4,3,2,1,0:T(8,128)(2,1)S(1)} copy-done((bf16[1,1,3,128,128]{4,3,2,1,0:T(8,128)(2,1)S(1)}, bf16[1,1,3,128,128]{4,3,2,1,0:T(8,128)(2,1)}, u32[]{:S(2)}) %copy-start.4) | copy-done | bytes 98328
  38.8 0.0 copy-start.6
  38.8 0.7 %copy-done.6 = s32[1,8]{1,0:T(1,128)S(1)} copy-done((s32[1,8]{1,0:T(1,128)S(1)}, s32[1,8]{1,0:T(1,128)}, u32[]{:S(2)}) %copy-start.6) | copy-done | bytes 56
  39.4 0.0 copy-start.7
  39.4 0.7 %copy-done.7 = s32[1,1,3]{2,1,0:T(1,128)S(1)} copy-done((s32[1,1,3]{2,1,0:T(1,128)S(1)}, s32[1,1,3]{2,1,0:T(1,128)}, u32[]{:S(2)}) %copy-start.7) | copy-done | bytes 36
  40.1 8.2 %apply.1 = bf16[8,256,256]{2,1,0:T(8,128)(2,1)} custom-call(s32[1,8]{1,0:T(1,128)S(1)} %copy-done.6, s32[8,7]{1,0:T(8,128)S(1)} %fusion.3.table_ref, s32[1,3]{1,0:T(1,128)S(1)} %bitcast.37, s32[1,1]{1,0:T(1,128)S(6)} %copy.17.m2l_count_ref, s32[1,128]{1,0:T(1,128)S(1)} %reshape.51.recv_ref, f32[1,128]{1,0:T(1,128)S(1)} %broadcast_select_fusion.weight_ref, ...), custom_call_target="tpu_custom_call" | custom-call | flops 2400000000 | bytes 12582912 | tf_op jit(solution)/shard_map/apply/pallas_call | solution.py:200
  (4 shorter events, 0.0 us)
Async XLA Ops:
  0.8 1.2 %copy-start = (bf16[1,8,256,256]{3,2,1,0:T(8,128)(2,1)S(1)}, bf16[1,8,256,256]{3,2,1,0:T(8,128)(2,1)}, u32[]{:S(2)}) copy-start(bf16[1,8,256,256]{3,2,1,0:T(8,128)(2,1)} %param.14) | copy-start | bytes 3145732
  2.0 1.0 %copy-start.2 = (bf16[1,8,128,256]{3,2,1,0:T(8,128)(2,1)S(1)}, bf16[1,8,128,256]{3,2,1,0:T(8,128)(2,1)}, u32[]{:S(2)}) copy-start(bf16[1,8,128,256]{3,2,1,0:T(8,128)(2,1)} %param.19) | copy-start | bytes 1572868
  3.0 0.7 %copy-start.5 = (s32[1,8]{1,0:T(1,128)S(1)}, s32[1,8]{1,0:T(1,128)}, u32[]{:S(2)}) copy-start(s32[1,8]{1,0:T(1,128)} %count_ref.3) | copy-start | bytes 100
  5.6 17.3 %all-to-all-start = ((bf16[4,256,256]{2,1,0:T(8,128)(2,1)}), bf16[4,256,256]{2,1,0:T(8,128)(2,1)S(1)}, u32[]{:S(2)}, u32[]{:S(2)}) async-start(bf16[4,256,256]{2,1,0:T(8,128)(2,1)} %pack.1), calls=%async_computation | async-start | bytes 1048576 | tf_op jit(solution)/shard_map/all_to_all | solution.py:186
  12.9 14.4 %collective-permute-start.1 = (bf16[3,256,256]{2,1,0:T(8,128)(2,1)S(1)}, bf16[3,256,256]{2,1,0:T(8,128)(2,1)S(1)}, u32[]{:S(2)}, u32[]{:S(2)}) collective-permute-start(bf16[3,256,256]{2,1,0:T(8,128)(2,1)S(1)} %get-tuple-element.5), channel_id=1, source_target_pairs={{1,2},{2,1},{5,6},{6,5},{9,10},{10,9},{13,14},{14,13},{17,18},{18,... | collective-permute-start | bytes 1179656 | tf_op jit(solution)/shard_map/ppermute | solution.py:171
  13.6 22.0 %collective-permute-start = (bf16[3,256,256]{2,1,0:T(8,128)(2,1)S(1)}, bf16[3,256,256]{2,1,0:T(8,128)(2,1)S(1)}, u32[]{:S(2)}, u32[]{:S(2)}) collective-permute-start(bf16[3,256,256]{2,1,0:T(8,128)(2,1)S(1)} %get-tuple-element.6), channel_id=1, source_target_pairs={{0,1},{1,0},{2,3},{3,2},{4,5},{5,4},{6,7},{7,6},{8,9},{9,8},{10,11... | collective-permute-start | bytes 1179656 | tf_op jit(solution)/shard_map/ppermute | solution.py:169
  22.9 12.7 %collective-permute-start.3 = (bf16[4,64,256]{2,1,0:T(8,128)(2,1)S(1)}, bf16[4,64,256]{2,1,0:T(8,128)(2,1)S(1)}, u32[]{:S(2)}, u32[]{:S(2)}) collective-permute-start(bf16[4,64,256]{2,1,0:T(8,128)(2,1)S(1)} %get-tuple-element.7), channel_id=1, source_target_pairs={{4,0},{8,4},{12,8},{16,12},{20,16},{24,20},{28,24},{5,1},{9,5},{13... | collective-permute-start | bytes 393224 | tf_op jit(solution)/shard_map/ppermute | solution.py:189
  24.2 11.4 %collective-permute-start.2 = (bf16[4,64,256]{2,1,0:T(8,128)(2,1)S(1)}, bf16[4,64,256]{2,1,0:T(8,128)(2,1)S(1)}, u32[]{:S(2)}, u32[]{:S(2)}) collective-permute-start(bf16[4,64,256]{2,1,0:T(8,128)(2,1)S(1)} %get-tuple-element.8), channel_id=1, source_target_pairs={{0,4},{4,8},{8,12},{12,16},{16,20},{20,24},{24,28},{1,5},{5,9},{9,... | collective-permute-start | bytes 393224 | tf_op jit(solution)/shard_map/ppermute | solution.py:188
  35.6 1.2 %copy-start.1 = (bf16[1,8,256,256]{3,2,1,0:T(8,128)(2,1)S(1)}, bf16[1,8,256,256]{3,2,1,0:T(8,128)(2,1)}, u32[]{:S(2)}) copy-start(bf16[1,8,256,256]{3,2,1,0:T(8,128)(2,1)} %param.14) | copy-start | bytes 3145732
  36.8 1.0 %copy-start.3 = (bf16[1,8,256,128]{3,2,1,0:T(8,128)(2,1)S(1)}, bf16[1,8,256,128]{3,2,1,0:T(8,128)(2,1)}, u32[]{:S(2)}) copy-start(bf16[1,8,256,128]{3,2,1,0:T(8,128)(2,1)} %param.23) | copy-start | bytes 1572868
  37.9 0.9 %copy-start.4 = (bf16[1,1,3,128,128]{4,3,2,1,0:T(8,128)(2,1)S(1)}, bf16[1,1,3,128,128]{4,3,2,1,0:T(8,128)(2,1)}, u32[]{:S(2)}) copy-start(bf16[1,1,3,128,128]{4,3,2,1,0:T(8,128)(2,1)} %param.22) | copy-start | bytes 294916
  38.8 0.7 %copy-start.6 = (s32[1,8]{1,0:T(1,128)S(1)}, s32[1,8]{1,0:T(1,128)}, u32[]{:S(2)}) copy-start(s32[1,8]{1,0:T(1,128)} %count_ref.3) | copy-start | bytes 100
  39.4 0.7 %copy-start.7 = (s32[1,1,3]{2,1,0:T(1,128)S(1)}, s32[1,1,3]{2,1,0:T(1,128)}, u32[]{:S(2)}) copy-start(s32[1,1,3]{2,1,0:T(1,128)} %param.20) | copy-start | bytes 40

commit v2 on v1

v2 whole, which is shorter than its diff:
```python
import functools

import jax
import jax.numpy as jnp
from jax import lax
from jax.experimental import pallas as pl
from jax.experimental.pallas import tpu as pltpu
from jax.sharding import PartitionSpec as P

REACH = 3
MIB = 1 << 20
F32 = jnp.float32
BF16 = jnp.bfloat16
INT = jnp.int32
COST = pl.CostEstimate(flops=1, bytes_accessed=1, transcendentals=0)


def dot(a, b):
    return jnp.dot(a, b, preferred_element_type=F32)


def live_rows(count, leaf_size, fields):
    return lax.broadcasted_iota(INT, (leaf_size, fields), 0) < count


def masked_leaf(x, count):
    rows, fields = x.shape
    live = jnp.where(live_rows(count, rows // 4, fields), 1.0, 0.0).astype(BF16)
    return (x.reshape(4, rows // 4, fields) * live[None]).reshape(rows, fields)


def column(values):
    width = values.shape[-1]
    wide = values.astype(F32).reshape(-1, 1, width)
    shape = (wide.shape[0], width, width)
    same = lax.broadcasted_iota(INT, shape, 1) == lax.broadcasted_iota(INT, shape, 2)
    return jnp.sum(jnp.where(same, wide, 0.0), axis=2, keepdims=True).reshape(-1, 1)


def row(col):
    n = col.shape[0]
    same = lax.broadcasted_iota(INT, (n, n), 0) == lax.broadcasted_iota(INT, (n, n), 1)
    return jnp.sum(jnp.where(same, col, 0.0), axis=0, keepdims=True)


def load(pairs, sems):
    copies = [pltpu.make_async_copy(a, b, sems.at[i]) for i, (a, b) in enumerate(pairs)]
    for copy in copies:
        copy.start()
    return copies


def box_of(place, boxes):
    return lax.rem(place, boxes)


def pack_kernel(square, *refs):
    place_hbm, count_hbm, send_hbm, x_hbm, source_hbm = refs[:5]
    outs, (place_ref, count_ref, send_ref, x_ref, source_ref, sems) = refs[5:-6], refs[-6:]
    pair_ref, other_ref = outs[:2]
    leaves, rows, fields = x_ref.shape
    leaf_size = rows // 4
    sides, boxes, slots = send_ref.shape
    q = source_ref.shape[1]
    copies = load(
        [
            (place_hbm, place_ref),
            (count_hbm, count_ref),
            (x_hbm.at[0], x_ref),
            (send_hbm.at[0, 0], send_ref),
            (source_hbm.at[0], source_ref),
        ],
        sems,
    )
    for copy in copies[:4]:
        copy.wait()
    me = box_of(place_ref[0], boxes)
    for l in range(leaves):
        x_ref[l] = masked_leaf(x_ref[l], count_ref[0, l])

    last = leaves - REACH
    odd = lax.rem(me, 2)
    for i in range(REACH):
        pair_ref[i] = x_ref[(1 - odd) * last + i]
        other_ref[i] = x_ref[odd * last + i]

    flip = me if square else 0
    index = [send_ref[s, pl.ds(r ^ flip, 1), :] for s in range(sides) for r in range(boxes)]
    send = column(jnp.concatenate(index, axis=0)).astype(INT)
    part = 4 * slots
    moment_at = []
    if square:
        across_ref, own_ref, self_ref = outs[2:]
        targets = [(self_ref, 0), (across_ref, q + sides * part), (own_ref, q), (across_ref, q)]
        moment_at = [across_ref.at[0:q], own_ref.at[0:q]]
    else:
        targets = [(outs[2].at[o], 0) for o in range(boxes)]
        moment_at = [outs[2].at[o, sides * part :] for o in range(boxes)]
    total = sides * boxes * slots
    element = lax.broadcasted_iota(INT, (total, leaves * leaf_size), 1)
    pick = jnp.where(element == send, 1.0, 0.0).astype(BF16)
    for c in range(4):
        comp = x_ref[:, c * leaf_size : (c + 1) * leaf_size, :]
        got = dot(pick, comp.reshape(leaves * leaf_size, fields)).astype(BF16)
        for s in range(sides):
            for r, (ref, base) in enumerate(targets):
                at = (s * boxes + r) * slots
                to = base + s * part + c * slots
                ref[to : to + slots, :] = got[at : at + slots]
    copies[4].wait()
    blocks = jnp.concatenate([source_ref[l] for l in range(leaves)], axis=1)
    moment = dot(blocks, x_ref[...].reshape(leaves * rows, fields)).astype(BF16)
    for ref in moment_at:
        ref[...] = moment


def local_kernel(
    square,
    place_hbm,
    count_hbm,
    idx_hbm,
    live_hbm,
    recv_hbm,
    recv_count_hbm,
    weight_hbm,
    x_hbm,
    near_hbm,
    acc_ref,
    rows_ref,
    near_ref,
    place_ref,
    count_ref,
    idx_ref,
    live_ref,
    recv_ref,
    recv_count_ref,
    weight_ref,
    src_ref,
    sems,
    near_sems,
):
    leaves, rows, fields = acc_ref.shape
    near_slots = idx_ref.shape[0]
    sides, boxes, slots = recv_ref.shape
    copies = load(
        [
            (place_hbm, place_ref),
            (count_hbm, count_ref),
            (x_hbm.at[0], src_ref.at[0:leaves]),
            (idx_hbm, idx_ref),
            (live_hbm, live_ref),
            (recv_hbm.at[0, 0], recv_ref),
            (recv_count_hbm.at[0, 0], recv_count_ref),
            (weight_hbm.at[0, 0], weight_ref),
        ],
        sems,
    )
    near_copies = load([(near_hbm.at[0, l], near_ref.at[l]) for l in range(leaves)], near_sems)
    src_ref[leaves] = jnp.zeros((rows, fields), BF16)
    for copy in copies:
        copy.wait()
    for l in range(leaves):
        src_ref[l] = masked_leaf(src_ref[l], count_ref[0, l])

    me = box_of(place_ref[0], boxes)
    flip = me if square else 0
    weights, targets = [], []
    for s in range(sides):
        for r in range(boxes):
            b = r ^ flip
            live = lax.broadcasted_iota(INT, (1, slots), 1) < recv_count_ref[s, b]
            weights.append(jnp.where(live, weight_ref[s, pl.ds(b, 1), :], 0.0))
            targets.append(recv_ref[s, pl.ds(b, 1), :])
    weight = row(column(jnp.concatenate(weights, axis=0)))
    upper = weight.astype(BF16).astype(F32)
    rows_ref[0:1, :] = row(column(jnp.concatenate(targets, axis=0)))
    rows_ref[1:2, :] = upper
    rows_ref[2:3, :] = weight - upper

    start = me * leaves
    for l in range(leaves):
        if l % 4 == 0:
            for copy in near_copies[l : l + 4]:
                copy.wait()
        blocks, sources = [], []
        for s in range(near_slots):
            at = idx_ref[s, 0, l] - start
            used = (s < live_ref[0, l]) & (at >= 0) & (at < leaves)
            blocks.append(near_ref[l, s])
            sources.append(src_ref[jnp.where(used, at, leaves)])
        acc_ref[l] = dot(jnp.concatenate(blocks, axis=1), jnp.concatenate(sources, axis=0))


def final_kernel(square, *refs):
    (
        place_hbm,
        count_hbm,
        idx_hbm,
        live_hbm,
        m2l_hbm,
        m2l_count_hbm,
        near_hbm,
        translate_hbm,
        evaluate_hbm,
        acc_ref,
        rows_ref,
        first_ref,
        direct_ref,
        turned_ref,
        left_ref,
        right_ref,
    ) = refs[:16]
    (
        out_hbm,
        place_ref,
        count_ref,
        idx_ref,
        live_ref,
        m2l_ref,
        m2l_count_ref,
        translate_ref,
        evaluate_ref,
        moment_ref,
        near_ref,
        halo_ref,
        out_ref,
        part_ref,
        sems,
        near_sems,
        out_sems,
    ) = refs[-17:]
    moments = refs[16:-17]
    leaves, rows, fields = acc_ref.shape
    leaf_size = rows // 4
    near_slots = idx_ref.shape[0]
    boxes, part, _ = left_ref.shape
    slots = part // 4
    q = translate_ref.shape[1]
    copies = load(
        [
            (place_hbm, place_ref),
            (idx_hbm, idx_ref),
            (live_hbm, live_ref),
            (count_hbm, count_ref),
            (m2l_hbm, m2l_ref),
            (m2l_count_hbm, m2l_count_ref),
            (translate_hbm.at[0, 0], translate_ref),
            (evaluate_hbm.at[0], evaluate_ref),
        ],
        sems,
    )
    zero_block = leaves * near_slots
    near_ref[zero_block] = jnp.zeros((rows, rows), BF16)
    halo_ref[2 * REACH] = jnp.zeros((rows, fields), BF16)
    for i in range(REACH):
        halo_ref[i] = first_ref[i]
    if square:
        own_ref, across_ref, beyond_ref = moments
        for r, (ref, at) in enumerate(
            [(own_ref, 0), (across_ref, 0), (beyond_ref, 0), (beyond_ref, q + 2 * part)]
        ):
            moment_ref[r] = ref[at : at + q]
    else:
        for r in range(boxes):
            moment_ref[r] = moments[0][r, 2 * part :]
    for copy in copies[:3]:
        copy.wait()

    place = place_ref[0]
    me = box_of(place, boxes)
    odd = lax.rem(me, 2)
    start = me * leaves
    low = REACH + (1 - odd) * REACH
    high = odd * REACH - leaves
    outer = [l for l in range(leaves) if l < REACH or l >= leaves - REACH]

    def slot(l, s):
        at = idx_ref[s, 0, l] - start
        used = (s < live_ref[0, l]) & ((at < 0) | (at >= leaves))
        return used, at + jnp.where(at < 0, low, high)

    def block_copy(l, s):
        n = l * near_slots + s
        return pltpu.make_async_copy(near_hbm.at[0, l, s], near_ref.at[n], near_sems.at[n])

    for l in outer:
        for s in range(near_slots):

            @pl.when(slot(l, s)[0])
            def _(l=l, s=s):
                block_copy(l, s).start()

    slot_total = rows_ref.shape[1]
    element = lax.broadcasted_iota(INT, (leaves * leaf_size, slot_total), 0)
    hit = element == rows_ref[0:1, :].astype(INT)
    spread = jnp.concatenate(
        [jnp.where(hit, rows_ref[i : i + 1, :], 0.0).astype(BF16) for i in (1, 2)], axis=1
    )
    for c in range(4):
        comp = [
            ref[:, c * slots : (c + 1) * slots, :].reshape(boxes * slots, fields)
            for ref in (left_ref, right_ref)
        ]
        sums = dot(spread, jnp.concatenate(comp + comp, axis=0))
        sums = sums if c < 2 else -sums
        part_ref[:, c * leaf_size : (c + 1) * leaf_size, :] = sums.reshape(
            leaves, leaf_size, fields
        )

    for copy in copies[3:]:
        copy.wait()
    flip = me if square else 0
    local = jnp.zeros((q, fields), F32)
    for t in range(translate_ref.shape[0]):
        moment = moment_ref[m2l_ref[0, 0, t] ^ flip]
        moment = jnp.where(t < m2l_count_ref[0, 0], moment.astype(F32), 0.0).astype(BF16)
        local += dot(translate_ref[t], moment)
    local = local.astype(BF16)

    relayed = place >= boxes
    for flag, ref in ((relayed, turned_ref), (jnp.logical_not(relayed), direct_ref)):

        @pl.when(flag)
        def _(ref=ref):
            for i in range(REACH):
                halo_ref[REACH + i] = ref[i]

    for l in outer:
        for s in range(near_slots):

            @pl.when(slot(l, s)[0])
            def _(l=l, s=s):
                block_copy(l, s).wait()

    stores = []
    for l in range(leaves):
        blocks, sources = [evaluate_ref[l]], [local]
        if l in outer:
            for s in range(near_slots):
                used, at = slot(l, s)
                blocks.append(near_ref[jnp.where(used, l * near_slots + s, zero_block)])
                sources.append(halo_ref[jnp.where(used, at, 2 * REACH)])
        total = dot(jnp.concatenate(blocks, axis=1), jnp.concatenate(sources, axis=0))
        total = (total + acc_ref[l] + part_ref[l]).reshape(4, leaf_size, fields)
        live = live_rows(count_ref[0, l], leaf_size, fields)
        out_ref[l] = jnp.where(live[None], total, 0.0).astype(BF16).reshape(rows, fields)
        stores.append(pltpu.make_async_copy(out_ref.at[l], out_hbm.at[l], out_sems.at[l]))
        stores[-1].start()
    for store in stores:
        store.wait()


def vmem():
    return pl.BlockSpec(memory_space=pltpu.VMEM)


def hbm():
    return pl.BlockSpec(memory_space=pltpu.MemorySpace.HBM)


def pin(x):
    return pltpu.with_memory_space_constraint(x, pltpu.MemorySpace.HBM)


def shards(
    traces,
    elem_count,
    near_idx,
    near_count,
    near_blocks,
    source_map,
    m2l_idx,
    m2l_count,
    translate,
    evaluate,
    send_idx,
    recv_idx,
    recv_count,
    couple_weight,
):
    leaves, rows, fields = traces.shape[1:]
    q = source_map.shape[2]
    sides, _, slots = send_idx.shape[2:]
    near_slots = near_idx.shape[2]
    groups = lax.axis_size("iface")
    boxes = lax.axis_size("sub")
    part = 4 * slots
    slot_total = sides * boxes * slots
    square = boxes == 4
    place = lax.axis_index("sub")
    if square:
        place = place + boxes * lax.rem(lax.axis_index("iface"), 2)
    place = place.reshape(1)

    params = pltpu.CompilerParams(vmem_limit_bytes=24 * MIB)
    piece = jax.ShapeDtypeStruct((REACH, rows, fields), BF16)
    if square:
        shapes = [(q + 2 * sides * part, fields), (q + sides * part, fields), (sides * part, fields)]
    else:
        shapes = [(boxes, sides * part + q, fields)]
    to_pair, to_other, *packed = pl.pallas_call(
        functools.partial(pack_kernel, square),
        out_shape=[piece, piece] + [jax.ShapeDtypeStruct(shape, BF16) for shape in shapes],
        in_specs=[hbm()] * 5,
        out_specs=[vmem()] * (2 + len(shapes)),
        scratch_shapes=[
            pltpu.SMEM((1,), INT),
            pltpu.SMEM((1, leaves), INT),
            pltpu.VMEM(send_idx.shape[2:], INT),
            pltpu.VMEM((leaves, rows, fields), BF16),
            pltpu.VMEM((leaves, q, rows), BF16),
            pltpu.SemaphoreType.DMA((5,)),
        ],
        compiler_params=params,
        cost_estimate=COST,
        name="pack",
    )(place, pin(elem_count), pin(send_idx), pin(traces), pin(source_map))

    def flips(bit):
        return [(b, b ^ bit) for b in range(boxes) if b ^ bit < boxes]

    def clusters(chosen, sub_pairs):
        return [(g * boxes + i, g * boxes + j) for g in chosen for i, j in sub_pairs]

    axes = ("iface", "sub")
    every = range(groups)
    across = [(b, b + 1) for b in range(1, boxes - 1, 2)]
    across = across + [(j, i) for i, j in across]
    up = [(g, g + 1) for g in range(groups - 1)]
    down = [(g + 1, g) for g in range(groups - 1)]
    near_at = pin(near_idx.transpose(2, 0, 1))

    def local_sums(place):
        return pl.pallas_call(
            functools.partial(local_kernel, square),
            out_shape=(
                jax.ShapeDtypeStruct((leaves, rows, fields), F32),
                jax.ShapeDtypeStruct((8, slot_total), F32),
            ),
            in_specs=[hbm()] * 9,
            out_specs=(vmem(),) * 2,
            scratch_shapes=[
                pltpu.VMEM(near_blocks.shape[1:], BF16),
                pltpu.SMEM((1,), INT),
                pltpu.SMEM((1, leaves), INT),
                pltpu.SMEM((near_slots, 1, leaves), INT),
                pltpu.SMEM((1, leaves), INT),
                pltpu.VMEM((sides, boxes, slots), INT),
                pltpu.SMEM((sides, boxes), INT),
                pltpu.VMEM((sides, boxes, slots), F32),
                pltpu.VMEM((leaves + 1, rows, fields), BF16),
                pltpu.SemaphoreType.DMA((8,)),
                pltpu.SemaphoreType.DMA((leaves,)),
            ],
            compiler_params=params,
            cost_estimate=COST,
            name="local",
        )(
            place,
            pin(elem_count),
            near_at,
            pin(near_count),
            pin(recv_idx),
            pin(recv_count),
            pin(couple_weight),
            pin(traces),
            pin(near_blocks),
        )

    if square:
        to_across, own, mine = packed
        from_across = lax.ppermute(to_across, "sub", flips(1))
        first = lax.ppermute(to_pair, "sub", flips(1))
        hop = lax.ppermute(to_other, axes, clusters(every[1::2], [(1, 3), (2, 0)]))
        direct = lax.ppermute(to_other, axes, clusters(every[::2], across))
        both = jnp.concatenate([own, from_across[: q + sides * part]], axis=0)
        beyond = lax.ppermute(both, "sub", flips(2))
        turned = lax.ppermute(
            hop, axes, clusters(every[1::2], [(3, 2), (0, 1)])
        )
        acc, slot_rows = local_sums(place)
        beyond = lax.optimization_barrier((beyond, slot_rows))[0]
        owned = []
        for s in range(sides):
            at = [(mine, 0), (from_across, q + sides * part), (beyond, q), (beyond, 2 * q + sides * part)]
            owned.append(
                jnp.concatenate([x[i + s * part : i + (s + 1) * part] for x, i in at], axis=0)
            )
        to_next, to_prev = (x.reshape(boxes, part, fields) for x in (owned[1], owned[0]))
        moments = (own, from_across, beyond)
    else:
        first = lax.ppermute(to_pair, "sub", flips(1))
        direct = lax.ppermute(to_other, "sub", across)
        turned = direct
        acc, slot_rows = local_sums(place)
        owned = lax.all_to_all(packed[0], "sub", split_axis=0, concat_axis=0, tiled=True)
        to_prev, to_next = owned[:, :part], owned[:, part : 2 * part]
        moments = (owned,)
    left = lax.ppermute(to_next, "iface", up)
    right = lax.ppermute(to_prev, "iface", down)

    out = pl.pallas_call(
        functools.partial(final_kernel, square),
        out_shape=jax.ShapeDtypeStruct((leaves, rows, fields), BF16),
        in_specs=[hbm()] * 9 + [vmem()] * (7 + len(moments)),
        out_specs=hbm(),
        scratch_shapes=[
            pltpu.SMEM((1,), INT),
            pltpu.SMEM((1, leaves), INT),
            pltpu.SMEM((near_slots, 1, leaves), INT),
            pltpu.SMEM((1, leaves), INT),
            pltpu.SMEM((1, 1, translate.shape[2]), INT),
            pltpu.SMEM((1, 1), INT),
            pltpu.VMEM(translate.shape[2:], BF16),
            pltpu.VMEM((leaves, rows, q), BF16),
            pltpu.VMEM((boxes, q, fields), BF16),
            pltpu.VMEM((leaves * near_slots + 1, rows, rows), BF16),
            pltpu.VMEM((2 * REACH + 1, rows, fields), BF16),
            pltpu.VMEM((leaves, rows, fields), BF16),
            pltpu.VMEM((leaves, rows, fields), F32),
            pltpu.SemaphoreType.DMA((8,)),
            pltpu.SemaphoreType.DMA((leaves * near_slots,)),
            pltpu.SemaphoreType.DMA((leaves,)),
        ],
        compiler_params=params,
        cost_estimate=COST,
        name="final",
    )(
        place,
        pin(elem_count),
        near_at,
        pin(near_count),
        pin(m2l_idx),
        m2l_count,
        pin(near_blocks),
        pin(translate),
        pin(evaluate),
        acc,
        slot_rows,
        first,
        direct,
        turned,
        left,
        right,
        *moments,
    )
    return out[None]


def solution(mesh):
    def split(rank):
        return P("iface", "sub", *(None,) * (rank - 2))

    return jax.shard_map(
        shards,
        mesh=mesh,
        in_specs=tuple(split(rank) for rank in (4, 2, 3, 2, 5, 4, 3, 2, 5, 4, 5, 5, 4, 5)),
        out_specs=split(4),
        check_vma=False,
    )
```

time: 48.9 us -> 36.9 us (0.75)
  the two profiles are of different devices: /device:TPU:0 before, /device:TPU:19 now
where the time goes in v2:
time: 36.9 us; the launch traced here: 36.6 us
  Pallas kernels  13.8 us (37%)
  starting transfers between devices  13.8 us (37%)
  waiting for transfers between devices  8.11 us (22%)
  between operations  0.79 us (2%)
    pallas_call x1, Pallas kernels, shards(): pl.pallas_call(functools.partial(final_kernel, square), out_shape=jax.Sha...  6 us
    pallas_call x1, Pallas kernels, local_sums(): pl.pallas_call(functools.partial(local_kernel, square), out_shape=(jax.Sh...  5.5 us
    ppermute x1, starting transfers between devices, shards(): left = lax.ppermute(to_next, 'iface', up)  5.1 us
    ppermute x1, waiting for transfers between devices, shards(): right = lax.ppermute(to_prev, 'iface', down)  3.68 us
    ppermute x1, starting transfers between devices, shards(): hop = lax.ppermute(to_other, axes, clusters(every[1::2], [(1, 3), (2, 0)]))  3.16 us
    ppermute x1, waiting for transfers between devices, shards(): beyond = lax.ppermute(both, 'sub', flips(2))  2.84 us
    pallas_call x1, Pallas kernels, shards(): pl.pallas_call(functools.partial(pack_kernel, square), out_shape=[piece,...  2.29 us
    ppermute x1, starting transfers between devices, shards(): right = lax.ppermute(to_prev, 'iface', down)  1.92 us
  transfers between devices with their start and end apart: 8, of which 3 were waited for; matrix products, arithmetic and copies ran while one was open for 0% of the time, Pallas kernels for 15%

profile of v2, /device:TPU:19, one launch (start us, length us, event | category | flops | bytes accessed | tf_op | source)
XLA Modules:
  0.0 36.6 jit_solution(14655215303635023330)
XLA Ops:
  0.0 2.3 %pack.1 = (bf16[3,256,256]{2,1,0:T(8,128)(2,1)S(1)}, bf16[3,256,256]{2,1,0:T(8,128)(2,1)S(1)}, bf16[384,256]{1,0:T(8,128)(2,1)S(1)}, bf16[256,256]{1,0:T(8,128)(2,1)S(1)}, bf16[128,256]{1,0:T(8,128)(2,1)S(1)}) custom-call(s32[1]{0:T(128)} %bitcast.place_hbm.refs_0_, s32[1,8]{1,0:T(1,128)} %refs_1_.3, s32[1,1,2,4,16]{4,3,2,1,0:T(4,128)} %refs_2_.1, ...), custom_call_target="tpu_custom_call" | custom-call | flops 1 | bytes 1 | tf_op jit(solution)/shard_map/pack/pallas_call | solution.py:401
  2.3 0.3 collective-permute-start.4
  2.6 3.2 %collective-permute-start.2 = (bf16[3,256,256]{2,1,0:T(8,128)(2,1)S(1)}, bf16[3,256,256]{2,1,0:T(8,128)(2,1)S(1)}, u32[]{:S(2)}, u32[]{:S(2)}) collective-permute-start(bf16[3,256,256]{2,1,0:T(8,128)(2,1)S(1)} %get-tuple-element.16), channel_id=1, source_target_pairs={{5,7},{6,4},{13,15},{14,12},{21,23},{22,20},{29,31},{30,28}} | collective-permute-start | bytes 1179656 | tf_op jit(solution)/shard_map/ppermute | solution.py:474
  5.8 0.7 %collective-permute-start.1 = (bf16[3,256,256]{2,1,0:T(8,128)(2,1)S(1)}, bf16[3,256,256]{2,1,0:T(8,128)(2,1)S(1)}, u32[]{:S(2)}, u32[]{:S(2)}) collective-permute-start(bf16[3,256,256]{2,1,0:T(8,128)(2,1)S(1)} %get-tuple-element.16), channel_id=1, source_target_pairs={{1,2},{2,1},{9,10},{10,9},{17,18},{18,17},{25,26},{26,25}} | collective-permute-start | bytes 1179656 | tf_op jit(solution)/shard_map/ppermute | solution.py:475
  6.5 0.1 collective-permute-start
  6.6 1.6 %collective-permute-done.4.refs_17_ = bf16[384,256]{1,0:T(8,128)(2,1)S(1)} collective-permute-done((bf16[384,256]{1,0:T(8,128)(2,1)S(1)}, bf16[384,256]{1,0:T(8,128)(2,1)S(1)}, u32[]{:S(2)}, u32[]{:S(2)}) %collective-permute-start.4) | collective-permute-done | bytes 196640 | tf_op jit(solution)/shard_map/ppermute | solution.py:472
  8.2 1.3 %collective-permute-start.5 = (bf16[512,256]{1,0:T(8,128)(2,1)S(1)}, bf16[512,256]{1,0:T(8,128)(2,1)S(1)}, u32[]{:S(2)}, u32[]{:S(2)}) collective-permute-start(bf16[512,256]{1,0:T(8,128)(2,1)S(1)} %pad_maximum_fusion), channel_id=1, source_target_pairs={{0,2},{1,3},{2,0},{3,1},{4,6},{5,7},{6,4},{7,5},{8,10},{9,11},{10,... | collective-permute-start | bytes 786440 | tf_op jit(solution)/shard_map/ppermute | solution.py:477
  9.5 5.5 %local.1 = (f32[8,256,256]{2,1,0:T(8,128)S(1)}, f32[8,128]{1,0:T(8,128)S(1)}) custom-call(s32[1]{0:T(128)} %bitcast.place_hbm.refs_0_, s32[1,8]{1,0:T(1,128)} %refs_1_.3, s32[7,1,8]{2,1,0:T(1,128)} %bitcast.7, s32[1,8]{1,0:T(1,128)} %refs_3_.3, s32[1,1,2,4,16]{4,3,2,1,0:T(4,128)} %recv_hbm.1, s32[1,1,2,4]{3,2,1,0:T(2,128)} %recv_count_hbm.1, ...), custom_call_target="tpu_custom_call" | custom-call | flops 1 | bytes 1 | tf_op jit(solution)/shard_map/local/pallas_call | solution.py:434
  15.0 0.0 collective-permute-done.2
  15.0 1.3 %collective-permute-start.3 = (bf16[3,256,256]{2,1,0:T(8,128)(2,1)S(1)}, bf16[3,256,256]{2,1,0:T(8,128)(2,1)S(1)}, u32[]{:S(2)}, u32[]{:S(2)}) collective-permute-start(bf16[3,256,256]{2,1,0:T(8,128)(2,1)S(1)} %collective-permute-done.2), channel_id=1, source_target_pairs={{7,6},{4,5},{15,14},{12,13},{23,22},{20,21},{31,30},{28,29}} | collective-permute-start | bytes 1179656 | tf_op jit(solution)/shard_map/ppermute | solution.py:478
  16.3 2.8 %collective-permute-done.5.refs_18_ = bf16[512,256]{1,0:T(8,128)(2,1)S(1)} collective-permute-done((bf16[512,256]{1,0:T(8,128)(2,1)S(1)}, bf16[512,256]{1,0:T(8,128)(2,1)S(1)}, u32[]{:S(2)}, u32[]{:S(2)}) %collective-permute-start.5) | collective-permute-done | bytes 262176 | tf_op jit(solution)/shard_map/ppermute | solution.py:477
  19.2 5.1 %collective-permute-start.6 = (bf16[4,64,256]{2,1,0:T(8,128)(2,1)S(1)}, bf16[4,64,256]{2,1,0:T(8,128)(2,1)S(1)}, u32[]{:S(2)}, u32[]{:S(2)}) collective-permute-start(bf16[4,64,256]{2,1,0:T(8,128)(2,1)S(1)} %bitcast.5), channel_id=1, source_target_pairs={{0,4},{4,8},{8,12},{12,16},{16,20},{20,24},{24,28},{1,5},{5,9},{9,... | collective-permute-start | bytes 393224 | tf_op jit(solution)/shard_map/ppermute | solution.py:499
  24.3 1.9 %collective-permute-start.7 = (bf16[4,64,256]{2,1,0:T(8,128)(2,1)S(1)}, bf16[4,64,256]{2,1,0:T(8,128)(2,1)S(1)}, u32[]{:S(2)}, u32[]{:S(2)}) collective-permute-start(bf16[4,64,256]{2,1,0:T(8,128)(2,1)S(1)} %bitcast.6), channel_id=1, source_target_pairs={{4,0},{8,4},{12,8},{16,12},{20,16},{24,20},{28,24},{5,1},{9,5},{13... | collective-permute-start | bytes 393224 | tf_op jit(solution)/shard_map/ppermute | solution.py:500
  26.9 0.0 collective-permute-done.refs_11_
  26.9 0.0 collective-permute-done.1.refs_12_
  26.9 0.0 collective-permute-done.6.refs_14_
  26.9 3.7 %collective-permute-done.7.refs_15_ = bf16[4,64,256]{2,1,0:T(8,128)(2,1)S(1)} collective-permute-done((bf16[4,64,256]{2,1,0:T(8,128)(2,1)S(1)}, bf16[4,64,256]{2,1,0:T(8,128)(2,1)S(1)}, u32[]{:S(2)}, u32[]{:S(2)}) %collective-permute-start.7) | collective-permute-done | bytes 131104 | tf_op jit(solution)/shard_map/ppermute | solution.py:500
  30.6 0.0 collective-permute-done.3.refs_13_
  30.6 6.0 %final.1 = bf16[8,256,256]{2,1,0:T(8,128)(2,1)} custom-call(s32[1]{0:T(128)} %bitcast.place_hbm.refs_0_, s32[1,8]{1,0:T(1,128)} %refs_1_.3, s32[7,1,8]{2,1,0:T(1,128)} %bitcast.8, s32[1,8]{1,0:T(1,128)} %refs_3_.3, s32[1,1,3]{2,1,0:T(1,128)} %refs_4_.3, s32[1,1]{1,0:T(1,128)S(6)} %copy.15.refs_5_, bf16[1,8,7,256,256]{4,3,2,1,0:T(8,128)(2,1)} %refs_6_.1, ...), custom_call_target="tpu_custom_call" | custom-call | flops 1 | bytes 1 | tf_op jit(solution)/shard_map/final/pallas_call | solution.py:502
  (7 shorter events, 0.1 us)
Async XLA Ops:
  2.3 5.8 %collective-permute-start.4 = (bf16[384,256]{1,0:T(8,128)(2,1)S(1)}, bf16[384,256]{1,0:T(8,128)(2,1)S(1)}, u32[]{:S(2)}, u32[]{:S(2)}) collective-permute-start(bf16[384,256]{1,0:T(8,128)(2,1)S(1)} %get-tuple-element.18), channel_id=1, source_target_pairs={{0,1},{1,0},{2,3},{3,2},{4,5},{5,4},{6,7},{7,6},{8,9},{9,8},{10,11... | collective-permute-start | bytes 589832 | tf_op jit(solution)/shard_map/ppermute | solution.py:472
  2.6 12.4 %collective-permute-start.2 = (bf16[3,256,256]{2,1,0:T(8,128)(2,1)S(1)}, bf16[3,256,256]{2,1,0:T(8,128)(2,1)S(1)}, u32[]{:S(2)}, u32[]{:S(2)}) collective-permute-start(bf16[3,256,256]{2,1,0:T(8,128)(2,1)S(1)} %get-tuple-element.16), channel_id=1, source_target_pairs={{5,7},{6,4},{13,15},{14,12},{21,23},{22,20},{29,31},{30,28}} | collective-permute-start | bytes 1179656 | tf_op jit(solution)/shard_map/ppermute | solution.py:474
  5.8 21.1 %collective-permute-start.1 = (bf16[3,256,256]{2,1,0:T(8,128)(2,1)S(1)}, bf16[3,256,256]{2,1,0:T(8,128)(2,1)S(1)}, u32[]{:S(2)}, u32[]{:S(2)}) collective-permute-start(bf16[3,256,256]{2,1,0:T(8,128)(2,1)S(1)} %get-tuple-element.16), channel_id=1, source_target_pairs={{1,2},{2,1},{9,10},{10,9},{17,18},{18,17},{25,26},{26,25}} | collective-permute-start | bytes 1179656 | tf_op jit(solution)/shard_map/ppermute | solution.py:475
  6.5 20.4 %collective-permute-start = (bf16[3,256,256]{2,1,0:T(8,128)(2,1)S(1)}, bf16[3,256,256]{2,1,0:T(8,128)(2,1)S(1)}, u32[]{:S(2)}, u32[]{:S(2)}) collective-permute-start(bf16[3,256,256]{2,1,0:T(8,128)(2,1)S(1)} %get-tuple-element.15), channel_id=1, source_target_pairs={{0,1},{1,0},{2,3},{3,2},{4,5},{5,4},{6,7},{7,6},{8,9},{9,8},{10,11... | collective-permute-start | bytes 1179656 | tf_op jit(solution)/shard_map/ppermute | solution.py:473
  8.2 11.0 %collective-permute-start.5 = (bf16[512,256]{1,0:T(8,128)(2,1)S(1)}, bf16[512,256]{1,0:T(8,128)(2,1)S(1)}, u32[]{:S(2)}, u32[]{:S(2)}) collective-permute-start(bf16[512,256]{1,0:T(8,128)(2,1)S(1)} %pad_maximum_fusion), channel_id=1, source_target_pairs={{0,2},{1,3},{2,0},{3,1},{4,6},{5,7},{6,4},{7,5},{8,10},{9,11},{10,... | collective-permute-start | bytes 786440 | tf_op jit(solution)/shard_map/ppermute | solution.py:477
  15.0 15.6 %collective-permute-start.3 = (bf16[3,256,256]{2,1,0:T(8,128)(2,1)S(1)}, bf16[3,256,256]{2,1,0:T(8,128)(2,1)S(1)}, u32[]{:S(2)}, u32[]{:S(2)}) collective-permute-start(bf16[3,256,256]{2,1,0:T(8,128)(2,1)S(1)} %collective-permute-done.2), channel_id=1, source_target_pairs={{7,6},{4,5},{15,14},{12,13},{23,22},{20,21},{31,30},{28,29}} | collective-permute-start | bytes 1179656 | tf_op jit(solution)/shard_map/ppermute | solution.py:478
  19.2 7.7 %collective-permute-start.6 = (bf16[4,64,256]{2,1,0:T(8,128)(2,1)S(1)}, bf16[4,64,256]{2,1,0:T(8,128)(2,1)S(1)}, u32[]{:S(2)}, u32[]{:S(2)}) collective-permute-start(bf16[4,64,256]{2,1,0:T(8,128)(2,1)S(1)} %bitcast.5), channel_id=1, source_target_pairs={{0,4},{4,8},{8,12},{12,16},{16,20},{20,24},{24,28},{1,5},{5,9},{9,... | collective-permute-start | bytes 393224 | tf_op jit(solution)/shard_map/ppermute | solution.py:499
  24.3 6.3 %collective-permute-start.7 = (bf16[4,64,256]{2,1,0:T(8,128)(2,1)S(1)}, bf16[4,64,256]{2,1,0:T(8,128)(2,1)S(1)}, u32[]{:S(2)}, u32[]{:S(2)}) collective-permute-start(bf16[4,64,256]{2,1,0:T(8,128)(2,1)S(1)} %bitcast.6), channel_id=1, source_target_pairs={{4,0},{8,4},{12,8},{16,12},{20,16},{24,20},{28,24},{5,1},{9,5},{13... | collective-permute-start | bytes 393224 | tf_op jit(solution)/shard_map/ppermute | solution.py:500

commit v3 on v2

v3 whole, which is shorter than its diff:
```python
import functools

import jax
import jax.numpy as jnp
from jax import lax
from jax.experimental import pallas as pl
from jax.experimental.pallas import tpu as pltpu
from jax.sharding import PartitionSpec as P

REACH = 3
MIB = 1 << 20
F32 = jnp.float32
BF16 = jnp.bfloat16
INT = jnp.int32
GROUP = 4
COST = pl.CostEstimate(flops=1, bytes_accessed=1, transcendentals=0)


def dot(a, b):
    return jnp.dot(a, b, preferred_element_type=F32)


def live_rows(count, leaf_size, fields):
    return lax.broadcasted_iota(INT, (leaf_size, fields), 0) < count


def masked_leaf(x, count):
    rows, fields = x.shape
    live = jnp.where(live_rows(count, rows // 4, fields), 1.0, 0.0).astype(BF16)
    return (x.reshape(4, rows // 4, fields) * live[None]).reshape(rows, fields)


def column(values):
    width = values.shape[-1]
    wide = values.astype(F32).reshape(-1, 1, width)
    shape = (wide.shape[0], width, width)
    same = lax.broadcasted_iota(INT, shape, 1) == lax.broadcasted_iota(INT, shape, 2)
    return jnp.sum(jnp.where(same, wide, 0.0), axis=2, keepdims=True).reshape(-1, 1)


def row(col):
    n = col.shape[0]
    same = lax.broadcasted_iota(INT, (n, n), 0) == lax.broadcasted_iota(INT, (n, n), 1)
    return jnp.sum(jnp.where(same, col, 0.0), axis=0, keepdims=True)


def load(pairs, sems):
    copies = [pltpu.make_async_copy(a, b, sems.at[i]) for i, (a, b) in enumerate(pairs)]
    for copy in copies:
        copy.start()
    return copies


def box_of(place, boxes):
    return lax.rem(place, boxes)


def met_side(place, boxes):
    return jnp.where(place < boxes, 1, 0)


def edge_kernel(boxes, place_hbm, count_hbm, x_hbm, pair_ref, other_ref, place_ref, count_ref, x_ref, sems):
    last = x_hbm.shape[1] - REACH
    copies = load(
        [
            (place_hbm, place_ref),
            (count_hbm, count_ref),
            (x_hbm.at[0, 0:REACH], x_ref.at[0:REACH]),
            (x_hbm.at[0, last:], x_ref.at[REACH:]),
        ],
        sems,
    )
    for copy in copies:
        copy.wait()
    odd = lax.rem(box_of(place_ref[0], boxes), 2)
    for i in range(REACH):
        for ref, upper in ((pair_ref, 1 - odd), (other_ref, odd)):
            ref[i] = masked_leaf(x_ref[upper * REACH + i], count_ref[0, upper * last + i])


def pack_kernel(
    after_hbm,
    place_hbm,
    count_hbm,
    send_hbm,
    x_hbm,
    source_hbm,
    chunk_ref,
    place_ref,
    count_ref,
    send_ref,
    x_ref,
    source_ref,
    sems,
):
    leaves, rows, fields = x_ref.shape
    leaf_size = rows // 4
    sides, boxes, slots = send_ref.shape
    copies = load(
        [
            (place_hbm, place_ref),
            (count_hbm, count_ref),
            (send_hbm.at[0, 0], send_ref),
            (x_hbm.at[0], x_ref),
            (source_hbm.at[0], source_ref),
        ],
        sems,
    )
    for copy in copies[:3]:
        copy.wait()
    met = met_side(place_ref[0], boxes)
    send = jnp.concatenate([send_ref[met], send_ref[1 - met]], axis=0)
    send = column(send).astype(INT)
    part = 4 * slots
    total = sides * boxes * slots
    element = lax.broadcasted_iota(INT, (total, leaves * leaf_size), 1)
    pick = jnp.where(element == send, 1.0, 0.0).astype(BF16)
    copies[3].wait()
    for l in range(leaves):
        x_ref[l] = masked_leaf(x_ref[l], count_ref[0, l])
    for c in range(4):
        comp = x_ref[:, c * leaf_size : (c + 1) * leaf_size, :]
        got = dot(pick, comp.reshape(leaves * leaf_size, fields)).astype(BF16)
        for s in range(sides):
            for o in range(boxes):
                at = (s * boxes + o) * slots
                to = s * part + c * slots
                chunk_ref[o, to : to + slots, :] = got[at : at + slots]
    copies[4].wait()
    blocks = jnp.concatenate([source_ref[l] for l in range(leaves)], axis=1)
    moment = dot(blocks, x_ref[...].reshape(leaves * rows, fields)).astype(BF16)
    for o in range(boxes):
        chunk_ref[o, sides * part :, :] = moment


def near_kernel(
    place_hbm,
    count_hbm,
    idx_hbm,
    live_hbm,
    recv_hbm,
    recv_count_hbm,
    weight_hbm,
    x_hbm,
    near_hbm,
    first_hbm,
    acc_ref,
    rows_ref,
    place_ref,
    count_ref,
    idx_ref,
    live_ref,
    recv_ref,
    recv_count_ref,
    weight_ref,
    near_ref,
    src_ref,
    sems,
    near_sems,
):
    leaves, rows, fields = acc_ref.shape
    leaf_size = rows // 4
    near_slots = idx_ref.shape[0]
    sides, boxes, slots = recv_ref.shape
    copies = load(
        [
            (place_hbm, place_ref),
            (count_hbm, count_ref),
            (recv_hbm.at[0, 0], recv_ref),
            (recv_count_hbm.at[0, 0], recv_count_ref),
            (weight_hbm.at[0, 0], weight_ref),
            (idx_hbm, idx_ref),
            (live_hbm, live_ref),
            (x_hbm.at[0], src_ref.at[0:leaves]),
            (first_hbm, src_ref.at[leaves : leaves + REACH]),
        ],
        sems,
    )
    near_copies = load([(near_hbm.at[0, l], near_ref.at[l]) for l in range(leaves)], near_sems)
    zero_leaf = leaves + REACH
    src_ref[zero_leaf] = jnp.zeros((rows, fields), BF16)
    for copy in copies[:7]:
        copy.wait()

    met = met_side(place_ref[0], boxes)
    weights = []
    for s in (met, 1 - met):
        for b in range(boxes):
            live = lax.broadcasted_iota(INT, (1, slots), 1) < recv_count_ref[s, b]
            weights.append(jnp.where(live, weight_ref[s, b : b + 1, :], 0.0))
    weight = row(column(jnp.concatenate(weights, axis=0)))
    target = jnp.concatenate([recv_ref[met], recv_ref[1 - met]], axis=0)
    target = row(column(target))
    upper = weight.astype(BF16).astype(F32)
    rows_ref[0:1, :] = target
    rows_ref[1:2, :] = upper
    rows_ref[2:3, :] = weight - upper

    copies[7].wait()
    copies[8].wait()
    for l in range(leaves):
        src_ref[l] = masked_leaf(src_ref[l], count_ref[0, l])
    me = box_of(place_ref[0], boxes)
    odd = lax.rem(me, 2) == 1
    start = me * leaves
    for l in range(leaves):
        if l % GROUP == 0:
            for copy in near_copies[l : l + GROUP]:
                copy.wait()
        blocks, sources = [], []
        for s in range(near_slots):
            at = idx_ref[s, 0, l] - start
            pair = jnp.where(odd, at < 0, at >= leaves)
            own = (at >= 0) & (at < leaves)
            at = at + jnp.where(pair & odd, leaves + REACH, 0)
            used = (s < live_ref[0, l]) & (own | pair)
            blocks.append(near_ref[l, s])
            sources.append(src_ref[jnp.where(used, at, zero_leaf)])
        acc_ref[l] = dot(jnp.concatenate(blocks, axis=1), jnp.concatenate(sources, axis=0))


def final_kernel(
    square,
    place_hbm,
    count_hbm,
    idx_hbm,
    live_hbm,
    m2l_hbm,
    m2l_count_hbm,
    near_hbm,
    translate_hbm,
    evaluate_hbm,
    acc_ref,
    rows_ref,
    direct_ref,
    turned_ref,
    met_ref,
    other_ref,
    owned_ref,
    out_hbm,
    place_ref,
    count_ref,
    idx_ref,
    live_ref,
    m2l_ref,
    m2l_count_ref,
    near_ref,
    translate_ref,
    evaluate_ref,
    halo_ref,
    out_ref,
    part_ref,
    sems,
    out_sems,
):
    leaves, rows, fields = out_ref.shape
    leaf_size = rows // 4
    near_slots = idx_ref.shape[0]
    boxes, part, _ = met_ref.shape
    slots = part // 4
    q = translate_ref.shape[1]
    copies = load(
        [
            (place_hbm, place_ref),
            (m2l_hbm, m2l_ref),
            (m2l_count_hbm, m2l_count_ref),
            (count_hbm, count_ref),
            (idx_hbm, idx_ref),
            (live_hbm, live_ref),
            (translate_hbm.at[0, 0], translate_ref),
            (evaluate_hbm.at[0], evaluate_ref),
        ],
        sems,
    )
    zero_leaf = REACH
    halo_ref[zero_leaf] = jnp.zeros((rows, fields), BF16)
    copies[0].wait()
    place = place_ref[0]
    me = box_of(place, boxes)
    odd = lax.rem(me, 2)
    edge = odd * (leaves - REACH)
    near_copy = pltpu.make_async_copy(near_hbm.at[0, pl.ds(edge, REACH)], near_ref, out_sems.at[0])
    near_copy.start()

    relayed = square & (place >= boxes)
    for flag, ref in ((relayed, turned_ref), (jnp.logical_not(relayed), direct_ref)):

        @pl.when(flag)
        def _(ref=ref):
            for i in range(REACH):
                halo_ref[i] = ref[i]

    slot_total = rows_ref.shape[1]
    element = lax.broadcasted_iota(INT, (leaves * leaf_size, slot_total), 0)
    hit = element == rows_ref[0:1, :].astype(INT)
    spread = jnp.concatenate(
        [jnp.where(hit, rows_ref[i : i + 1, :], 0.0).astype(BF16) for i in (1, 2)], axis=1
    )
    for c in range(4):
        comp = [
            ref[:, c * slots : (c + 1) * slots, :].reshape(boxes * slots, fields)
            for ref in (met_ref, other_ref)
        ]
        sums = dot(spread, jnp.concatenate(comp + comp, axis=0))
        sums = sums if c < 2 else -sums
        part_ref[:, c * leaf_size : (c + 1) * leaf_size, :] = sums.reshape(
            leaves, leaf_size, fields
        )

    for copy in copies[1:]:
        copy.wait()
    local = jnp.zeros((q, fields), F32)
    for t in range(translate_ref.shape[0]):
        moment = owned_ref[m2l_ref[0, 0, t], 2 * part :, :]
        moment = jnp.where(t < m2l_count_ref[0, 0], moment.astype(F32), 0.0).astype(BF16)
        local += dot(translate_ref[t], moment)
    local = local.astype(BF16)
    for l in range(leaves):
        part_ref[l] += dot(evaluate_ref[l], local) + acc_ref[l]

    near_copy.wait()
    start = me * leaves
    for i in range(REACH):
        l = edge + i
        blocks, sources = [], []
        for s in range(near_slots):
            at = idx_ref[s, 0, l] - start
            far = jnp.where(odd == 1, at >= leaves, at < 0)
            at = at + jnp.where(odd == 1, -leaves, REACH)
            blocks.append(near_ref[i, s])
            sources.append(halo_ref[jnp.where((s < live_ref[0, l]) & far, at, zero_leaf)])
        part_ref[l] += dot(jnp.concatenate(blocks, axis=1), jnp.concatenate(sources, axis=0))

    half = leaves // 2
    stores = []
    for l in range(leaves):
        total = part_ref[l].reshape(4, leaf_size, fields)
        live = live_rows(count_ref[0, l], leaf_size, fields)
        out_ref[l] = jnp.where(live[None], total, 0.0).astype(BF16).reshape(rows, fields)
        if l % half == half - 1:
            span = slice(l + 1 - half, l + 1)
            stores.append(
                pltpu.make_async_copy(out_ref.at[span], out_hbm.at[span], out_sems.at[1 + l // half])
            )
            stores[-1].start()
    for store in stores:
        store.wait()


def vmem():
    return pl.BlockSpec(memory_space=pltpu.VMEM)


def hbm():
    return pl.BlockSpec(memory_space=pltpu.MemorySpace.HBM)


def pin(x):
    return pltpu.with_memory_space_constraint(x, pltpu.MemorySpace.HBM)


def shards(
    traces,
    elem_count,
    near_idx,
    near_count,
    near_blocks,
    source_map,
    m2l_idx,
    m2l_count,
    translate,
    evaluate,
    send_idx,
    recv_idx,
    recv_count,
    couple_weight,
):
    leaves, rows, fields = traces.shape[1:]
    q = source_map.shape[2]
    sides, _, slots = send_idx.shape[2:]
    near_slots = near_idx.shape[2]
    groups = lax.axis_size("iface")
    boxes = lax.axis_size("sub")
    part = 4 * slots
    slot_total = sides * boxes * slots
    square = boxes == 4
    parity = lax.rem(lax.axis_index("iface"), 2)
    place = (lax.axis_index("sub") + boxes * parity).reshape(1)

    params = pltpu.CompilerParams(vmem_limit_bytes=24 * MIB)
    piece = jax.ShapeDtypeStruct((REACH, rows, fields), BF16)
    chunk = jax.ShapeDtypeStruct((boxes, sides * part + q, fields), BF16)
    to_pair, to_other = pl.pallas_call(
        functools.partial(edge_kernel, boxes),
        out_shape=[piece, piece],
        in_specs=[hbm()] * 3,
        out_specs=[vmem()] * 2,
        scratch_shapes=[
            pltpu.SMEM((1,), INT),
            pltpu.SMEM((1, leaves), INT),
            pltpu.VMEM((2 * REACH, rows, fields), BF16),
            pltpu.SemaphoreType.DMA((4,)),
        ],
        compiler_params=params,
        cost_estimate=COST,
        name="edges",
    )(place, pin(elem_count), pin(traces))
    chunks = pl.pallas_call(
        pack_kernel,
        out_shape=chunk,
        in_specs=[pl.BlockSpec(memory_space=pl.ANY)] + [hbm()] * 5,
        out_specs=vmem(),
        scratch_shapes=[
            pltpu.SMEM((1,), INT),
            pltpu.SMEM((1, leaves), INT),
            pltpu.VMEM(send_idx.shape[2:], INT),
            pltpu.VMEM((leaves, rows, fields), BF16),
            pltpu.VMEM((leaves, q, rows), BF16),
            pltpu.SemaphoreType.DMA((5,)),
        ],
        compiler_params=params,
        cost_estimate=COST,
        name="pack",
    )(to_pair, place, pin(elem_count), pin(send_idx), pin(traces), pin(source_map))

    def flips(bit):
        return [(b, b ^ bit) for b in range(boxes) if b ^ bit < boxes]

    def clusters(chosen, sub_pairs):
        return [(g * boxes + i, g * boxes + j) for g in chosen for i, j in sub_pairs]

    axes = ("iface", "sub")
    every = range(groups)
    across = [(b, b + 1) for b in range(1, boxes - 1, 2)]
    across = across + [(j, i) for i, j in across]
    owned = lax.all_to_all(chunks, "sub", split_axis=0, concat_axis=0, tiled=True)
    first = lax.ppermute(to_pair, "sub", flips(1))
    if square:
        hop = lax.ppermute(to_other, axes, clusters(every[1::2], [(1, 3), (2, 0)]))
        direct = lax.ppermute(to_other, axes, clusters(every[::2], across))
        turned = lax.ppermute(lax.optimization_barrier((hop, first))[0], axes, clusters(every[1::2], [(3, 2), (0, 1)]))
    else:
        direct = lax.ppermute(to_other, "sub", across)
        turned = direct
    near_at = pin(near_idx.transpose(2, 0, 1))
    slot_total = sides * boxes * slots
    acc, slot_rows = pl.pallas_call(
        near_kernel,
        out_shape=(
            jax.ShapeDtypeStruct((leaves, rows, fields), F32),
            jax.ShapeDtypeStruct((8, slot_total), F32),
        ),
        in_specs=[hbm()] * 10,
        out_specs=(vmem(), vmem()),
        scratch_shapes=[
            pltpu.SMEM((1,), INT),
            pltpu.SMEM((1, leaves), INT),
            pltpu.SMEM((near_slots, 1, leaves), INT),
            pltpu.SMEM((1, leaves), INT),
            pltpu.VMEM((sides, boxes, slots), INT),
            pltpu.SMEM((sides, boxes), INT),
            pltpu.VMEM((sides, boxes, slots), F32),
            pltpu.VMEM(near_blocks.shape[1:], BF16),
            pltpu.VMEM((leaves + REACH + 1, rows, fields), BF16),
            pltpu.SemaphoreType.DMA((9,)),
            pltpu.SemaphoreType.DMA((leaves,)),
        ],
        compiler_params=params,
        cost_estimate=COST,
        name="near",
    )(
        place,
        pin(elem_count),
        near_at,
        pin(near_count),
        pin(recv_idx),
        pin(recv_count),
        pin(couple_weight),
        pin(traces),
        pin(near_blocks),
        pin(first),
    )

    owned = lax.optimization_barrier((owned, slot_rows))[0]
    meet = [(g, g ^ 1) for g in range(groups) if g ^ 1 < groups]
    met = lax.ppermute(owned[:, :part], "iface", meet)
    turn = [(g, g + 1) for g in range(1, groups - 1, 2)]
    other = lax.ppermute(owned[:, part : 2 * part], "iface", turn + [(j, i) for i, j in turn])

    out = pl.pallas_call(
        functools.partial(final_kernel, square),
        out_shape=jax.ShapeDtypeStruct((leaves, rows, fields), BF16),
        in_specs=[hbm()] * 9 + [vmem()] * 7,
        out_specs=hbm(),
        scratch_shapes=[
            pltpu.SMEM((1,), INT),
            pltpu.SMEM((1, leaves), INT),
            pltpu.SMEM((near_slots, 1, leaves), INT),
            pltpu.SMEM((1, leaves), INT),
            pltpu.SMEM((1, 1, translate.shape[2]), INT),
            pltpu.SMEM((1, 1), INT),
            pltpu.VMEM((REACH,) + near_blocks.shape[2:], BF16),
            pltpu.VMEM(translate.shape[2:], BF16),
            pltpu.VMEM((leaves, rows, q), BF16),
            pltpu.VMEM((REACH + 1, rows, fields), BF16),
            pltpu.VMEM((leaves, rows, fields), BF16),
            pltpu.VMEM((leaves, rows, fields), F32),
            pltpu.SemaphoreType.DMA((8,)),
            pltpu.SemaphoreType.DMA((3,)),
        ],
        compiler_params=params,
        cost_estimate=COST,
        name="final",
    )(
        place,
        pin(elem_count),
        near_at,
        pin(near_count),
        pin(m2l_idx),
        m2l_count,
        pin(near_blocks),
        pin(translate),
        pin(evaluate),
        acc,
        slot_rows,
        direct,
        turned,
        met,
        other,
        owned,
    )
    return out[None]


def solution(mesh):
    def split(rank):
        return P("iface", "sub", *(None,) * (rank - 2))

    return jax.shard_map(
        shards,
        mesh=mesh,
        in_specs=tuple(split(rank) for rank in (4, 2, 3, 2, 5, 4, 3, 2, 5, 4, 5, 5, 4, 5)),
        out_specs=split(4),
        check_vma=False,
    )
```

time: 36.9 us -> 34.3 us (0.930)
  the two profiles are of different devices: /device:TPU:19 before, /device:TPU:1 now
where the time goes in v3:
time: 34.3 us; the launch traced here: 34 us
  Pallas kernels  15.2 us (44%)
  starting transfers between devices  14.8 us (43%)
  waiting for transfers between devices  3.2 us (9%)
  between operations  0.77 us (2%)
    pallas_call x1, Pallas kernels, shards(): pl.pallas_call(near_kernel, out_shape=(jax.ShapeDtypeStruct((leaves, rows...  5.52 us
    pallas_call x1, Pallas kernels, shards(): pl.pallas_call(functools.partial(final_kernel, square), out_shape=jax.Sha...  4.8 us
    ppermute x1, starting transfers between devices, shards(): lax.ppermute(lax.optimization_barrier((hop, first))[0], axes, clusters(ev...  4.14 us
    all_to_all x1, starting transfers between devices, shards(): lax.all_to_all(chunks, 'sub', split_axis=0, concat_axis=0, tiled=True)  4.13 us
    ppermute x1, waiting for transfers between devices, shards(): lax.ppermute(owned[:, part:2 * part], 'iface', turn + [(j, i) for i, j in...  3.18 us
    pallas_call x1, Pallas kernels, shards(): pl.pallas_call(pack_kernel, out_shape=chunk, in_specs=[pl.BlockSpec(memor...  2.95 us
    ppermute x1, starting transfers between devices, shards(): lax.ppermute(owned[:, part:2 * part], 'iface', turn + [(j, i) for i, j in...  2.36 us
    ppermute x1, starting transfers between devices, shards(): first = lax.ppermute(to_pair, 'sub', flips(1))  2.11 us
  transfers between devices with their start and end apart: 7, of which 1 were waited for; matrix products, arithmetic and copies ran while one was open for 0% of the time, Pallas kernels for 25%

profile of v3, /device:TPU:1, one launch (start us, length us, event | category | flops | bytes accessed | tf_op | source)
XLA Modules:
  0.0 34.0 jit_solution(6148457416101216818)
XLA Ops:
  0.0 1.9 %edges.1 = (bf16[3,256,256]{2,1,0:T(8,128)(2,1)S(1)}, bf16[3,256,256]{2,1,0:T(8,128)(2,1)}) custom-call(s32[1]{0:T(128)} %bitcast.place_hbm, s32[1,8]{1,0:T(1,128)} %count_hbm.7, bf16[1,8,256,256]{3,2,1,0:T(8,128)(2,1)} %x_hbm.5), custom_call_target="tpu_custom_call" | custom-call | flops 1 | bytes 1 | tf_op jit(solution)/shard_map/edges/pallas_call | solution.py:393
  1.9 2.1 %collective-permute-start = (bf16[3,256,256]{2,1,0:T(8,128)(2,1)S(1)}, bf16[3,256,256]{2,1,0:T(8,128)(2,1)S(1)}, u32[]{:S(2)}, u32[]{:S(2)}) collective-permute-start(bf16[3,256,256]{2,1,0:T(8,128)(2,1)S(1)} %get-tuple-element.11.after_hbm), channel_id=1, source_target_pairs={{0,1},{1,0},{2,3},{3,2},{4,5},{5,4},{6,7},{7,6},{8,9},{9,8},{10,11... | collective-permute-start | bytes 1179656 | tf_op jit(solution)/shard_map/ppermute | solution.py:437
  4.0 1.3 %collective-permute-start.2 = (bf16[3,256,256]{2,1,0:T(8,128)(2,1)}, bf16[3,256,256]{2,1,0:T(8,128)(2,1)}, u32[]{:S(2)}, u32[]{:S(2)}) collective-permute-start(bf16[3,256,256]{2,1,0:T(8,128)(2,1)} %get-tuple-element.14), channel_id=1, source_target_pairs={{5,7},{6,4},{13,15},{14,12},{21,23},{22,20},{29,31},{30,28}} | collective-permute-start | bytes 1179656 | tf_op jit(solution)/shard_map/ppermute | solution.py:439
  5.3 2.9 %pack.1 = bf16[4,256,256]{2,1,0:T(8,128)(2,1)} custom-call(bf16[3,256,256]{2,1,0:T(8,128)(2,1)S(1)} %get-tuple-element.11.after_hbm, s32[1]{0:T(128)} %bitcast.place_hbm, s32[1,8]{1,0:T(1,128)} %count_hbm.7, s32[1,1,2,4,16]{4,3,2,1,0:T(4,128)} %send_hbm.1, bf16[1,8,256,256]{3,2,1,0:T(8,128)(2,1)} %x_hbm.5, bf16[1,8,128,256]{3,2,1,0:T(8,128)(2,1)} %source_hbm.1), custom_call_target="tpu_custom_call" | custom-call | flops 1 | bytes 1 | tf_op jit(solution)/shard_map/pack/pallas_call | solution.py:408
  8.3 4.1 %all-to-all-start = ((bf16[4,256,256]{2,1,0:T(8,128)(2,1)}), bf16[4,256,256]{2,1,0:T(8,128)(2,1)S(1)}, u32[]{:S(2)}, u32[]{:S(2)}) async-start(bf16[4,256,256]{2,1,0:T(8,128)(2,1)} %pack.1), calls=%async_computation | async-start | bytes 1048576 | tf_op jit(solution)/shard_map/all_to_all | solution.py:436
  12.4 0.7 %collective-permute-start.1 = (bf16[3,256,256]{2,1,0:T(8,128)(2,1)}, bf16[3,256,256]{2,1,0:T(8,128)(2,1)S(1)}, u32[]{:S(2)}, u32[]{:S(2)}) collective-permute-start(bf16[3,256,256]{2,1,0:T(8,128)(2,1)} %get-tuple-element.14), channel_id=1, source_target_pairs={{1,2},{2,1},{9,10},{10,9},{17,18},{18,17},{25,26},{26,25}} | collective-permute-start | bytes 1179656 | tf_op jit(solution)/shard_map/ppermute | solution.py:440
  13.1 0.0 collective-permute-done.first_hbm
  13.1 0.0 copy-start
  13.1 0.0 collective-permute-done.2
  13.1 4.1 %collective-permute-start.3 = (bf16[3,256,256]{2,1,0:T(8,128)(2,1)}, bf16[3,256,256]{2,1,0:T(8,128)(2,1)S(1)}, u32[]{:S(2)}, u32[]{:S(2)}) collective-permute-start(bf16[3,256,256]{2,1,0:T(8,128)(2,1)} %collective-permute-done.2), channel_id=1, source_target_pairs={{7,6},{4,5},{15,14},{12,13},{23,22},{20,21},{31,30},{28,29}} | collective-permute-start | bytes 1179656 | tf_op jit(solution)/shard_map/ppermute | solution.py:441
  17.3 0.0 copy-done
  17.3 5.5 %near.1 = (f32[8,256,256]{2,1,0:T(8,128)S(1)}, f32[8,128]{1,0:T(8,128)S(1)}) custom-call(s32[1]{0:T(128)} %bitcast.place_hbm, s32[1,8]{1,0:T(1,128)} %count_hbm.7, s32[7,1,8]{2,1,0:T(1,128)} %bitcast.3, s32[1,8]{1,0:T(1,128)} %live_hbm.3, s32[1,1,2,4,16]{4,3,2,1,0:T(4,128)} %recv_hbm.1, s32[1,1,2,4]{3,2,1,0:T(2,128)} %recv_count_hbm.1, ...), custom_call_target="tpu_custom_call" | custom-call | flops 1 | bytes 1 | tf_op jit(solution)/shard_map/near/pallas_call | solution.py:447
  22.8 0.0 all-to-all-done.owned_ref
  22.9 2.4 %collective-permute-start.5 = (bf16[4,64,256]{2,1,0:T(8,128)(2,1)S(1)}, bf16[4,64,256]{2,1,0:T(8,128)(2,1)S(1)}, u32[]{:S(2)}, u32[]{:S(2)}) collective-permute-start(bf16[4,64,256]{2,1,0:T(8,128)(2,1)S(1)} %get-tuple-element.17), channel_id=1, source_target_pairs={{4,8},{12,16},{20,24},{8,4},{16,12},{24,20},{5,9},{13,17},{21,25},... | collective-permute-start | bytes 393224 | tf_op jit(solution)/shard_map/ppermute | solution.py:488
  25.2 0.1 collective-permute-start.4
  26.0 0.0 collective-permute-done.1.direct_ref
  26.0 3.2 %collective-permute-done.5.other_ref = bf16[4,64,256]{2,1,0:T(8,128)(2,1)S(1)} collective-permute-done((bf16[4,64,256]{2,1,0:T(8,128)(2,1)S(1)}, bf16[4,64,256]{2,1,0:T(8,128)(2,1)S(1)}, u32[]{:S(2)}, u32[]{:S(2)}) %collective-permute-start.5) | collective-permute-done | bytes 131104 | tf_op jit(solution)/shard_map/ppermute | solution.py:488
  29.1 0.0 collective-permute-done.4.met_ref
  29.1 0.0 collective-permute-done.3.turned_ref
  29.2 4.8 %final.1 = bf16[8,256,256]{2,1,0:T(8,128)(2,1)} custom-call(s32[1]{0:T(128)} %bitcast.place_hbm, s32[1,8]{1,0:T(1,128)} %count_hbm.7, s32[7,1,8]{2,1,0:T(1,128)} %bitcast.4, s32[1,8]{1,0:T(1,128)} %live_hbm.3, s32[1,1,3]{2,1,0:T(1,128)} %m2l_hbm.1, s32[1,1]{1,0:T(1,128)S(6)} %copy.15.m2l_count_hbm, bf16[1,8,7,256,256]{4,3,2,1,0:T(8,128)(2,1)} %near_hbm.3, ...), custom_call_target="tpu_custom_call" | custom-call | flops 1 | bytes 1 | tf_op jit(solution)/shard_map/final/pallas_call | solution.py:490
  (1 shorter events, 0.0 us)
Async XLA Ops:
  1.9 11.2 %collective-permute-start = (bf16[3,256,256]{2,1,0:T(8,128)(2,1)S(1)}, bf16[3,256,256]{2,1,0:T(8,128)(2,1)S(1)}, u32[]{:S(2)}, u32[]{:S(2)}) collective-permute-start(bf16[3,256,256]{2,1,0:T(8,128)(2,1)S(1)} %get-tuple-element.11.after_hbm), channel_id=1, source_target_pairs={{0,1},{1,0},{2,3},{3,2},{4,5},{5,4},{6,7},{7,6},{8,9},{9,8},{10,11... | collective-permute-start | bytes 1179656 | tf_op jit(solution)/shard_map/ppermute | solution.py:437
  4.0 9.1 %collective-permute-start.2 = (bf16[3,256,256]{2,1,0:T(8,128)(2,1)}, bf16[3,256,256]{2,1,0:T(8,128)(2,1)}, u32[]{:S(2)}, u32[]{:S(2)}) collective-permute-start(bf16[3,256,256]{2,1,0:T(8,128)(2,1)} %get-tuple-element.14), channel_id=1, source_target_pairs={{5,7},{6,4},{13,15},{14,12},{21,23},{22,20},{29,31},{30,28}} | collective-permute-start | bytes 1179656 | tf_op jit(solution)/shard_map/ppermute | solution.py:439
  8.3 14.5 %all-to-all-start = ((bf16[4,256,256]{2,1,0:T(8,128)(2,1)}), bf16[4,256,256]{2,1,0:T(8,128)(2,1)S(1)}, u32[]{:S(2)}, u32[]{:S(2)}) async-start(bf16[4,256,256]{2,1,0:T(8,128)(2,1)} %pack.1), calls=%async_computation | async-start | bytes 1048576 | tf_op jit(solution)/shard_map/all_to_all | solution.py:436
  12.4 13.5 %collective-permute-start.1 = (bf16[3,256,256]{2,1,0:T(8,128)(2,1)}, bf16[3,256,256]{2,1,0:T(8,128)(2,1)S(1)}, u32[]{:S(2)}, u32[]{:S(2)}) collective-permute-start(bf16[3,256,256]{2,1,0:T(8,128)(2,1)} %get-tuple-element.14), channel_id=1, source_target_pairs={{1,2},{2,1},{9,10},{10,9},{17,18},{18,17},{25,26},{26,25}} | collective-permute-start | bytes 1179656 | tf_op jit(solution)/shard_map/ppermute | solution.py:440
  13.1 4.2 %copy-start = (bf16[3,256,256]{2,1,0:T(8,128)(2,1)}, bf16[3,256,256]{2,1,0:T(8,128)(2,1)S(1)}, u32[]{:S(2)}) copy-start(bf16[3,256,256]{2,1,0:T(8,128)(2,1)S(1)} %collective-permute-done.first_hbm) | copy-start | bytes 1179652
  13.1 16.0 %collective-permute-start.3 = (bf16[3,256,256]{2,1,0:T(8,128)(2,1)}, bf16[3,256,256]{2,1,0:T(8,128)(2,1)S(1)}, u32[]{:S(2)}, u32[]{:S(2)}) collective-permute-start(bf16[3,256,256]{2,1,0:T(8,128)(2,1)} %collective-permute-done.2), channel_id=1, source_target_pairs={{7,6},{4,5},{15,14},{12,13},{23,22},{20,21},{31,30},{28,29}} | collective-permute-start | bytes 1179656 | tf_op jit(solution)/shard_map/ppermute | solution.py:441
  22.9 6.3 %collective-permute-start.5 = (bf16[4,64,256]{2,1,0:T(8,128)(2,1)S(1)}, bf16[4,64,256]{2,1,0:T(8,128)(2,1)S(1)}, u32[]{:S(2)}, u32[]{:S(2)}) collective-permute-start(bf16[4,64,256]{2,1,0:T(8,128)(2,1)S(1)} %get-tuple-element.17), channel_id=1, source_target_pairs={{4,8},{12,16},{20,24},{8,4},{16,12},{24,20},{5,9},{13,17},{21,25},... | collective-permute-start | bytes 393224 | tf_op jit(solution)/shard_map/ppermute | solution.py:488
  25.2 3.9 %collective-permute-start.4 = (bf16[4,64,256]{2,1,0:T(8,128)(2,1)S(1)}, bf16[4,64,256]{2,1,0:T(8,128)(2,1)S(1)}, u32[]{:S(2)}, u32[]{:S(2)}) collective-permute-start(bf16[4,64,256]{2,1,0:T(8,128)(2,1)S(1)} %get-tuple-element.18), channel_id=1, source_target_pairs={{0,4},{4,0},{8,12},{12,8},{16,20},{20,16},{24,28},{28,24},{1,5},{5... | collective-permute-start | bytes 393224 | tf_op jit(solution)/shard_map/ppermute | solution.py:486

commit v4 on v3

--- a/solution.py
+++ b/solution.py
@@ -85,7 +85,9 @@
     send_hbm,
     x_hbm,
     source_hbm,
-    chunk_ref,
+    met_ref,
+    other_ref,
+    moment_ref,
     place_ref,
     count_ref,
     send_ref,
@@ -111,7 +113,6 @@
     met = met_side(place_ref[0], boxes)
     send = jnp.concatenate([send_ref[met], send_ref[1 - met]], axis=0)
     send = column(send).astype(INT)
-    part = 4 * slots
     total = sides * boxes * slots
     element = lax.broadcasted_iota(INT, (total, leaves * leaf_size), 1)
     pick = jnp.where(element == send, 1.0, 0.0).astype(BF16)
@@ -121,16 +122,14 @@
     for c in range(4):
         comp = x_ref[:, c * leaf_size : (c + 1) * leaf_size, :]
         got = dot(pick, comp.reshape(leaves * leaf_size, fields)).astype(BF16)
-        for s in range(sides):
+        for s, ref in enumerate((met_ref, other_ref)):
             for o in range(boxes):
                 at = (s * boxes + o) * slots
-                to = s * part + c * slots
-                chunk_ref[o, to : to + slots, :] = got[at : at + slots]
+                ref[o, c * slots : (c + 1) * slots, :] = got[at : at + slots]
     copies[4].wait()
     blocks = jnp.concatenate([source_ref[l] for l in range(leaves)], axis=1)
     moment = dot(blocks, x_ref[...].reshape(leaves * rows, fields)).astype(BF16)
-    for o in range(boxes):
-        chunk_ref[o, sides * part :, :] = moment
+    moment_ref[...] = moment
 
 
 def near_kernel(
@@ -220,7 +219,6 @@
 
 
 def final_kernel(
-    square,
     place_hbm,
     count_hbm,
     idx_hbm,
@@ -233,9 +231,6 @@
     acc_ref,
     rows_ref,
     direct_ref,
-    turned_ref,
-    met_ref,
-    other_ref,
     owned_ref,
     out_hbm,
     place_ref,
@@ -256,9 +251,10 @@
     leaves, rows, fields = out_ref.shape
     leaf_size = rows // 4
     near_slots = idx_ref.shape[0]
-    boxes, part, _ = met_ref.shape
+    boxes, chunk, _ = owned_ref.shape
+    q = translate_ref.shape[1]
+    part = (chunk - q) // 2
     slots = part // 4
-    q = translate_ref.shape[1]
     copies = load(
         [
             (place_hbm, place_ref),
@@ -282,13 +278,8 @@
     near_copy = pltpu.make_async_copy(near_hbm.at[0, pl.ds(edge, REACH)], near_ref, out_sems.at[0])
     near_copy.start()
 
-    relayed = square & (place >= boxes)
-    for flag, ref in ((relayed, turned_ref), (jnp.logical_not(relayed), direct_ref)):
-
-        @pl.when(flag)
-        def _(ref=ref):
-            for i in range(REACH):
-                halo_ref[i] = ref[i]
+    for i in range(REACH):
+        halo_ref[i] = direct_ref[i]
 
     slot_total = rows_ref.shape[1]
     element = lax.broadcasted_iota(INT, (leaves * leaf_size, slot_total), 0)
@@ -298,8 +289,8 @@
     )
     for c in range(4):
         comp = [
-            ref[:, c * slots : (c + 1) * slots, :].reshape(boxes * slots, fields)
-            for ref in (met_ref, other_ref)
+            owned_ref[:, at : at + slots, :].reshape(boxes * slots, fields)
+            for at in (c * slots, part + c * slots)
         ]
         sums = dot(spread, jnp.concatenate(comp + comp, axis=0))
         sums = sums if c < 2 else -sums
@@ -315,8 +306,20 @@
         moment = jnp.where(t < m2l_count_ref[0, 0], moment.astype(F32), 0.0).astype(BF16)
         local += dot(translate_ref[t], moment)
     local = local.astype(BF16)
-    for l in range(leaves):
-        part_ref[l] += dot(evaluate_ref[l], local) + acc_ref[l]
+    def finish(l, total):
+        total = (total + acc_ref[l] + part_ref[l]).reshape(4, leaf_size, fields)
+        live = live_rows(count_ref[0, l], leaf_size, fields)
+        out_ref[l] = jnp.where(live[None], total, 0.0).astype(BF16).reshape(rows, fields)
+
+    rest = (1 - odd) * REACH
+    inner = leaves - REACH
+    for i in range(inner):
+        finish(rest + i, dot(evaluate_ref[rest + i], local))
+    stores = []
+    for at, size, sem in ((rest, inner, 1), (edge, REACH, 2)):
+        span = pl.ds(at, size)
+        stores.append(pltpu.make_async_copy(out_ref.at[span], out_hbm.at[span], out_sems.at[sem]))
+    stores[0].start()
 
     near_copy.wait()
     start = me * leaves
@@ -329,20 +332,10 @@
             at = at + jnp.where(odd == 1, -leaves, REACH)
             blocks.append(near_ref[i, s])
             sources.append(halo_ref[jnp.where((s < live_ref[0, l]) & far, at, zero_leaf)])
-        part_ref[l] += dot(jnp.concatenate(blocks, axis=1), jnp.concatenate(sources, axis=0))
-
-    half = leaves // 2
-    stores = []
-    for l in range(leaves):
-        total = part_ref[l].reshape(4, leaf_size, fields)
-        live = live_rows(count_ref[0, l], leaf_size, fields)
-        out_ref[l] = jnp.where(live[None], total, 0.0).astype(BF16).reshape(rows, fields)
-        if l % half == half - 1:
-            span = slice(l + 1 - half, l + 1)
-            stores.append(
-                pltpu.make_async_copy(out_ref.at[span], out_hbm.at[span], out_sems.at[1 + l // half])
-            )
-            stores[-1].start()
+        blocks.append(evaluate_ref[l])
+        sources.append(local)
+        finish(l, dot(jnp.concatenate(blocks, axis=1), jnp.concatenate(sources, axis=0)))
+    stores[1].start()
     for store in stores:
         store.wait()
 
@@ -383,13 +376,12 @@
     boxes = lax.axis_size("sub")
     part = 4 * slots
     slot_total = sides * boxes * slots
-    square = boxes == 4
     parity = lax.rem(lax.axis_index("iface"), 2)
     place = (lax.axis_index("sub") + boxes * parity).reshape(1)
 
     params = pltpu.CompilerParams(vmem_limit_bytes=24 * MIB)
     piece = jax.ShapeDtypeStruct((REACH, rows, fields), BF16)
-    chunk = jax.ShapeDtypeStruct((boxes, sides * part + q, fields), BF16)
+    toward = jax.ShapeDtypeStruct((boxes, part, fields), BF16)
     to_pair, to_other = pl.pallas_call(
         functools.partial(edge_kernel, boxes),
         out_shape=[piece, piece],
@@ -405,11 +397,11 @@
         cost_estimate=COST,
         name="edges",
     )(place, pin(elem_count), pin(traces))
-    chunks = pl.pallas_call(
+    to_met, to_turn, moment = pl.pallas_call(
         pack_kernel,
-        out_shape=chunk,
+        out_shape=(toward, toward, jax.ShapeDtypeStruct((q, fields), BF16)),
         in_specs=[pl.BlockSpec(memory_space=pl.ANY)] + [hbm()] * 5,
-        out_specs=vmem(),
+        out_specs=(vmem(),) * 3,
         scratch_shapes=[
             pltpu.SMEM((1,), INT),
             pltpu.SMEM((1, leaves), INT),
@@ -426,22 +418,19 @@
     def flips(bit):
         return [(b, b ^ bit) for b in range(boxes) if b ^ bit < boxes]
 
-    def clusters(chosen, sub_pairs):
-        return [(g * boxes + i, g * boxes + j) for g in chosen for i, j in sub_pairs]
-
-    axes = ("iface", "sub")
-    every = range(groups)
     across = [(b, b + 1) for b in range(1, boxes - 1, 2)]
     across = across + [(j, i) for i, j in across]
+    first = lax.ppermute(to_pair, "sub", flips(1))
+    meet = [(g, g ^ 1) for g in range(groups) if g ^ 1 < groups]
+    met = lax.ppermute(to_met, "iface", meet)
+    turn = [(g, g + 1) for g in range(1, groups - 1, 2)]
+    other = lax.ppermute(to_turn, "iface", turn + [(j, i) for i, j in turn])
+    to_other = lax.optimization_barrier((to_other, moment))[0]
+    direct = lax.ppermute(to_other, "sub", across)
+    carried = lax.optimization_barrier((moment, first))[0]
+    carried = jnp.broadcast_to(carried, (boxes, q, fields))
+    chunks = jnp.concatenate([met, other, carried], axis=1)
     owned = lax.all_to_all(chunks, "sub", split_axis=0, concat_axis=0, tiled=True)
-    first = lax.ppermute(to_pair, "sub", flips(1))
-    if square:
-        hop = lax.ppermute(to_other, axes, clusters(every[1::2], [(1, 3), (2, 0)]))
-        direct = lax.ppermute(to_other, axes, clusters(every[::2], across))
-        turned = lax.ppermute(lax.optimization_barrier((hop, first))[0], axes, clusters(every[1::2], [(3, 2), (0, 1)]))
-    else:
-        direct = lax.ppermute(to_other, "sub", across)
-        turned = direct
     near_at = pin(near_idx.transpose(2, 0, 1))
     slot_total = sides * boxes * slots
     acc, slot_rows = pl.pallas_call(
@@ -469,7 +458,7 @@
         cost_estimate=COST,
         name="near",
     )(
-        place,
+        lax.optimization_barrier((place, chunks))[0],
         pin(elem_count),
         near_at,
         pin(near_count),
@@ -481,16 +470,10 @@
         pin(first),
     )
 
-    owned = lax.optimization_barrier((owned, slot_rows))[0]
-    meet = [(g, g ^ 1) for g in range(groups) if g ^ 1 < groups]
-    met = lax.ppermute(owned[:, :part], "iface", meet)
-    turn = [(g, g + 1) for g in range(1, groups - 1, 2)]
-    other = lax.ppermute(owned[:, part : 2 * part], "iface", turn + [(j, i) for i, j in turn])
-
     out = pl.pallas_call(
-        functools.partial(final_kernel, square),
+        final_kernel,
         out_shape=jax.ShapeDtypeStruct((leaves, rows, fields), BF16),
-        in_specs=[hbm()] * 9 + [vmem()] * 7,
+        in_specs=[hbm()] * 9 + [vmem()] * 4,
         out_specs=hbm(),
         scratch_shapes=[
             pltpu.SMEM((1,), INT),
@@ -524,9 +507,6 @@
         acc,
         slot_rows,
         direct,
-        turned,
-        met,
-        other,
         owned,
     )
     return out[None]

time: 34.3 us -> 32.8 us (0.956)
  the two profiles are of different devices: /device:TPU:1 before, /device:TPU:9 now
where the time goes in v4:
time: 32.8 us; the launch traced here: 32.6 us
  Pallas kernels  13.4 us (41%)
  starting transfers between devices  9.56 us (29%)
  waiting for transfers between devices  8.07 us (25%)
  other arithmetic  0.83 us (3%)
  between operations  0.72 us (2%)
    pallas_call x1, Pallas kernels, shards(): pl.pallas_call(near_kernel, out_shape=(jax.ShapeDtypeStruct((leaves, rows...  5.51 us
    all_to_all x1, waiting for transfers between devices, shards(): lax.all_to_all(chunks, 'sub', split_axis=0, concat_axis=0, tiled=True)  5.3 us
    pallas_call x1, Pallas kernels, shards(): pl.pallas_call(final_kernel, out_shape=jax.ShapeDtypeStruct((leaves, rows...  4.5 us
    all_to_all x1, starting transfers between devices, shards(): lax.all_to_all(chunks, 'sub', split_axis=0, concat_axis=0, tiled=True)  3.47 us
    ppermute x1, starting transfers between devices, shards(): other = lax.ppermute(to_turn, 'iface', turn + [(j, i) for i, j in turn])  3.1 us
    pallas_call x1, Pallas kernels, shards(): pl.pallas_call(pack_kernel, out_shape=(toward, toward, jax.ShapeDtypeStru...  2.15 us
    ppermute x1, waiting for transfers between devices, shards(): first = lax.ppermute(to_pair, 'sub', flips(1))  1.79 us
    ppermute x1, starting transfers between devices, shards(): first = lax.ppermute(to_pair, 'sub', flips(1))  1.28 us
  transfers between devices with their start and end apart: 5, of which 3 were waited for; matrix products, arithmetic and copies ran while one was open for 3% of the time, Pallas kernels for 24%

profile of v4, /device:TPU:9, one launch (start us, length us, event | category | flops | bytes accessed | tf_op | source)
XLA Modules:
  0.0 32.6 jit_solution(6202531390252626967)
XLA Ops:
  0.0 1.2 %edges.1 = (bf16[3,256,256]{2,1,0:T(8,128)(2,1)S(1)}, bf16[3,256,256]{2,1,0:T(8,128)(2,1)S(1)}) custom-call(s32[1]{0:T(128)} %bitcast.place_hbm, s32[1,8]{1,0:T(1,128)} %count_hbm.7, bf16[1,8,256,256]{3,2,1,0:T(8,128)(2,1)} %x_hbm.5), custom_call_target="tpu_custom_call" | custom-call | flops 1 | bytes 1 | tf_op jit(solution)/shard_map/edges/pallas_call | solution.py:385
  1.2 1.3 %collective-permute-start.2 = (bf16[3,256,256]{2,1,0:T(8,128)(2,1)S(1)}, bf16[3,256,256]{2,1,0:T(8,128)(2,1)S(1)}, u32[]{:S(2)}, u32[]{:S(2)}) collective-permute-start(bf16[3,256,256]{2,1,0:T(8,128)(2,1)S(1)} %get-tuple-element.15.after_hbm), channel_id=1, source_target_pairs={{0,1},{1,0},{2,3},{3,2},{4,5},{5,4},{6,7},{7,6},{8,9},{9,8},{10,11... | collective-permute-start | bytes 1179656 | tf_op jit(solution)/shard_map/ppermute | solution.py:423
  2.5 2.1 %pack.1 = (bf16[4,64,256]{2,1,0:T(8,128)(2,1)S(1)}, bf16[4,64,256]{2,1,0:T(8,128)(2,1)S(1)}, bf16[128,256]{1,0:T(8,128)(2,1)S(1)}) custom-call(bf16[3,256,256]{2,1,0:T(8,128)(2,1)S(1)} %get-tuple-element.15.after_hbm, s32[1]{0:T(128)} %bitcast.place_hbm, s32[1,8]{1,0:T(1,128)} %count_hbm.7, s32[1,1,2,4,16]{4,3,2,1,0:T(4,128)} %send_hbm.1, ...), custom_call_target="tpu_custom_call" | custom-call | flops 1 | bytes 1 | tf_op jit(solution)/shard_map/pack/pallas_call | solution.py:400
  4.7 1.0 %collective-permute-start = (bf16[4,64,256]{2,1,0:T(8,128)(2,1)S(1)}, bf16[4,64,256]{2,1,0:T(8,128)(2,1)S(1)}, u32[]{:S(2)}, u32[]{:S(2)}) collective-permute-start(bf16[4,64,256]{2,1,0:T(8,128)(2,1)S(1)} %get-tuple-element.16), channel_id=1, source_target_pairs={{0,4},{4,0},{8,12},{12,8},{16,20},{20,16},{24,28},{28,24},{1,5},{5... | collective-permute-start | bytes 393224 | tf_op jit(solution)/shard_map/ppermute | solution.py:425
  5.7 3.1 %collective-permute-start.1 = (bf16[4,64,256]{2,1,0:T(8,128)(2,1)S(1)}, bf16[4,64,256]{2,1,0:T(8,128)(2,1)S(1)}, u32[]{:S(2)}, u32[]{:S(2)}) collective-permute-start(bf16[4,64,256]{2,1,0:T(8,128)(2,1)S(1)} %get-tuple-element.17), channel_id=1, source_target_pairs={{4,8},{12,16},{20,24},{8,4},{16,12},{24,20},{5,9},{13,17},{21,25},... | collective-permute-start | bytes 393224 | tf_op jit(solution)/shard_map/ppermute | solution.py:427
  8.8 0.7 %collective-permute-start.3 = (bf16[3,256,256]{2,1,0:T(8,128)(2,1)S(1)}, bf16[3,256,256]{2,1,0:T(8,128)(2,1)S(1)}, u32[]{:S(2)}, u32[]{:S(2)}) collective-permute-start(bf16[3,256,256]{2,1,0:T(8,128)(2,1)S(1)} %get-tuple-element.24), channel_id=1, source_target_pairs={{1,2},{2,1},{5,6},{6,5},{9,10},{10,9},{13,14},{14,13},{17,18},{18,... | collective-permute-start | bytes 1179656 | tf_op jit(solution)/shard_map/ppermute | solution.py:429
  9.5 1.8 %collective-permute-done.2.first_hbm = bf16[3,256,256]{2,1,0:T(8,128)(2,1)S(1)} collective-permute-done((bf16[3,256,256]{2,1,0:T(8,128)(2,1)S(1)}, bf16[3,256,256]{2,1,0:T(8,128)(2,1)S(1)}, u32[]{:S(2)}, u32[]{:S(2)}) %collective-permute-start.2) | collective-permute-done | bytes 393248 | tf_op jit(solution)/shard_map/ppermute | solution.py:423
  11.3 0.0 copy-start
  11.3 0.0 collective-permute-done
  11.3 1.0 %collective-permute-done.1 = bf16[4,64,256]{2,1,0:T(8,128)(2,1)S(1)} collective-permute-done((bf16[4,64,256]{2,1,0:T(8,128)(2,1)S(1)}, bf16[4,64,256]{2,1,0:T(8,128)(2,1)S(1)}, u32[]{:S(2)}, u32[]{:S(2)}) %collective-permute-start.1) | collective-permute-done | bytes 131104 | tf_op jit(solution)/shard_map/ppermute | solution.py:427
  12.3 0.0 copy-done
  12.3 0.8 %pad_maximum_fusion = bf16[4,256,256]{2,1,0:T(8,128)(2,1)} fusion(bf16[4,128,256]{2,1,0:T(8,128)(2,1)S(1)} %broadcast_in_dim.6, bf16[4,64,256]{2,1,0:T(8,128)(2,1)S(1)} %collective-permute-done.1, bf16[4,64,256]{2,1,0:T(8,128)(2,1)S(1)} %collective-permute-done), kind=kLoop, calls=%fused_computation | loop fusion | flops 1572864 | bytes 1048576 | tf_op jit(solution)/shard_map/concatenate | solution.py:432
  13.1 3.5 %all-to-all-start = ((bf16[4,256,256]{2,1,0:T(8,128)(2,1)}), bf16[4,256,256]{2,1,0:T(8,128)(2,1)S(1)}, u32[]{:S(2)}, u32[]{:S(2)}) async-start(bf16[4,256,256]{2,1,0:T(8,128)(2,1)} %pad_maximum_fusion), calls=%async_computation | async-start | bytes 1048576 | tf_op jit(solution)/shard_map/all_to_all | solution.py:433
  17.2 5.5 %near.1 = (f32[8,256,256]{2,1,0:T(8,128)S(1)}, f32[8,128]{1,0:T(8,128)S(1)}) custom-call(s32[1]{0:T(128)} %bitcast.place_hbm, s32[1,8]{1,0:T(1,128)} %count_hbm.7, s32[7,1,8]{2,1,0:T(1,128)} %bitcast.3, s32[1,8]{1,0:T(1,128)} %live_hbm.3, s32[1,1,2,4,16]{4,3,2,1,0:T(4,128)} %recv_hbm.1, s32[1,1,2,4]{3,2,1,0:T(2,128)} %recv_count_hbm.1, ...), custom_call_target="tpu_custom_call" | custom-call | flops 1 | bytes 1 | tf_op jit(solution)/shard_map/near/pallas_call | solution.py:436
  22.8 0.0 collective-permute-done.3.direct_ref
  22.8 5.3 %all-to-all-done.owned_ref = bf16[4,256,256]{2,1,0:T(8,128)(2,1)S(1)} async-done(((bf16[4,256,256]{2,1,0:T(8,128)(2,1)}), bf16[4,256,256]{2,1,0:T(8,128)(2,1)S(1)}, u32[]{:S(2)}, u32[]{:S(2)}) %all-to-all-start) | async-done | bytes 524320 | tf_op jit(solution)/shard_map/all_to_all | solution.py:433
  28.1 4.5 %final.1 = bf16[8,256,256]{2,1,0:T(8,128)(2,1)} custom-call(s32[1]{0:T(128)} %bitcast.place_hbm, s32[1,8]{1,0:T(1,128)} %count_hbm.7, s32[7,1,8]{2,1,0:T(1,128)} %bitcast.4, s32[1,8]{1,0:T(1,128)} %live_hbm.3, s32[1,1,3]{2,1,0:T(1,128)} %m2l_hbm.1, s32[1,1]{1,0:T(1,128)S(6)} %copy.15.m2l_count_hbm, bf16[1,8,7,256,256]{4,3,2,1,0:T(8,128)(2,1)} %near_hbm.3, ...), custom_call_target="tpu_custom_call" | custom-call | flops 1 | bytes 1 | tf_op jit(solution)/shard_map/final/pallas_call | solution.py:473
  (1 shorter events, 0.0 us)
Async XLA Ops:
  1.2 10.0 %collective-permute-start.2 = (bf16[3,256,256]{2,1,0:T(8,128)(2,1)S(1)}, bf16[3,256,256]{2,1,0:T(8,128)(2,1)S(1)}, u32[]{:S(2)}, u32[]{:S(2)}) collective-permute-start(bf16[3,256,256]{2,1,0:T(8,128)(2,1)S(1)} %get-tuple-element.15.after_hbm), channel_id=1, source_target_pairs={{0,1},{1,0},{2,3},{3,2},{4,5},{5,4},{6,7},{7,6},{8,9},{9,8},{10,11... | collective-permute-start | bytes 1179656 | tf_op jit(solution)/shard_map/ppermute | solution.py:423
  4.7 6.6 %collective-permute-start = (bf16[4,64,256]{2,1,0:T(8,128)(2,1)S(1)}, bf16[4,64,256]{2,1,0:T(8,128)(2,1)S(1)}, u32[]{:S(2)}, u32[]{:S(2)}) collective-permute-start(bf16[4,64,256]{2,1,0:T(8,128)(2,1)S(1)} %get-tuple-element.16), channel_id=1, source_target_pairs={{0,4},{4,0},{8,12},{12,8},{16,20},{20,16},{24,28},{28,24},{1,5},{5... | collective-permute-start | bytes 393224 | tf_op jit(solution)/shard_map/ppermute | solution.py:425
  5.7 6.6 %collective-permute-start.1 = (bf16[4,64,256]{2,1,0:T(8,128)(2,1)S(1)}, bf16[4,64,256]{2,1,0:T(8,128)(2,1)S(1)}, u32[]{:S(2)}, u32[]{:S(2)}) collective-permute-start(bf16[4,64,256]{2,1,0:T(8,128)(2,1)S(1)} %get-tuple-element.17), channel_id=1, source_target_pairs={{4,8},{12,16},{20,24},{8,4},{16,12},{24,20},{5,9},{13,17},{21,25},... | collective-permute-start | bytes 393224 | tf_op jit(solution)/shard_map/ppermute | solution.py:427
  8.8 14.0 %collective-permute-start.3 = (bf16[3,256,256]{2,1,0:T(8,128)(2,1)S(1)}, bf16[3,256,256]{2,1,0:T(8,128)(2,1)S(1)}, u32[]{:S(2)}, u32[]{:S(2)}) collective-permute-start(bf16[3,256,256]{2,1,0:T(8,128)(2,1)S(1)} %get-tuple-element.24), channel_id=1, source_target_pairs={{1,2},{2,1},{5,6},{6,5},{9,10},{10,9},{13,14},{14,13},{17,18},{18,... | collective-permute-start | bytes 1179656 | tf_op jit(solution)/shard_map/ppermute | solution.py:429
  11.3 1.0 %copy-start = (bf16[3,256,256]{2,1,0:T(8,128)(2,1)}, bf16[3,256,256]{2,1,0:T(8,128)(2,1)S(1)}, u32[]{:S(2)}) copy-start(bf16[3,256,256]{2,1,0:T(8,128)(2,1)S(1)} %collective-permute-done.2.first_hbm) | copy-start | bytes 1179652
  13.1 15.0 %all-to-all-start = ((bf16[4,256,256]{2,1,0:T(8,128)(2,1)}), bf16[4,256,256]{2,1,0:T(8,128)(2,1)S(1)}, u32[]{:S(2)}, u32[]{:S(2)}) async-start(bf16[4,256,256]{2,1,0:T(8,128)(2,1)} %pad_maximum_fusion), calls=%async_computation | async-start | bytes 1048576 | tf_op jit(solution)/shard_map/all_to_all | solution.py:433

commit v5 on v4

--- a/solution.py
+++ b/solution.py
@@ -311,33 +311,45 @@
         live = live_rows(count_ref[0, l], leaf_size, fields)
         out_ref[l] = jnp.where(live[None], total, 0.0).astype(BF16).reshape(rows, fields)
 
-    rest = (1 - odd) * REACH
+    start = me * leaves
     inner = leaves - REACH
-    for i in range(inner):
-        finish(rest + i, dot(evaluate_ref[rest + i], local))
-    stores = []
-    for at, size, sem in ((rest, inner, 1), (edge, REACH, 2)):
-        span = pl.ds(at, size)
-        stores.append(pltpu.make_async_copy(out_ref.at[span], out_hbm.at[span], out_sems.at[sem]))
-    stores[0].start()
-
-    near_copy.wait()
-    start = me * leaves
-    for i in range(REACH):
-        l = edge + i
-        blocks, sources = [], []
-        for s in range(near_slots):
-            at = idx_ref[s, 0, l] - start
-            far = jnp.where(odd == 1, at >= leaves, at < 0)
-            at = at + jnp.where(odd == 1, -leaves, REACH)
-            blocks.append(near_ref[i, s])
-            sources.append(halo_ref[jnp.where((s < live_ref[0, l]) & far, at, zero_leaf)])
-        blocks.append(evaluate_ref[l])
-        sources.append(local)
-        finish(l, dot(jnp.concatenate(blocks, axis=1), jnp.concatenate(sources, axis=0)))
-    stores[1].start()
-    for store in stores:
-        store.wait()
+
+    def sums(parity):
+        first_far = parity * inner
+        rest = (1 - parity) * REACH
+        stores = []
+
+        def store(at, size):
+            span = slice(at, at + size)
+            copy = pltpu.make_async_copy(
+                out_ref.at[span], out_hbm.at[span], out_sems.at[1 + len(stores)]
+            )
+            copy.start()
+            stores.append(copy)
+
+        for l in range(rest, rest + inner):
+            finish(l, dot(evaluate_ref[l], local))
+        store(rest, inner)
+        near_copy.wait()
+        for i in range(REACH):
+            l = first_far + i
+            blocks, sources = [], []
+            for s in range(near_slots):
+                at = idx_ref[s, 0, l] - start
+                far = at >= leaves if parity else at < 0
+                at = at + (-leaves if parity else REACH)
+                used = (s < live_ref[0, l]) & far
+                blocks.append(near_ref[i, s])
+                sources.append(halo_ref[jnp.where(used, at, zero_leaf)])
+            blocks.append(evaluate_ref[l])
+            sources.append(local)
+            finish(l, dot(jnp.concatenate(blocks, axis=1), jnp.concatenate(sources, axis=0)))
+            store(l, 1)
+        for copy in stores:
+            copy.wait()
+
+    for parity in (0, 1):
+        pl.when(odd == parity)(functools.partial(sums, parity))
 
 
 def vmem():
@@ -489,7 +501,7 @@
             pltpu.VMEM((leaves, rows, fields), BF16),
             pltpu.VMEM((leaves, rows, fields), F32),
             pltpu.SemaphoreType.DMA((8,)),
-            pltpu.SemaphoreType.DMA((3,)),
+            pltpu.SemaphoreType.DMA((2 + REACH,)),
         ],
         compiler_params=params,
         cost_estimate=COST,

time: 32.8 us -> 32.6 us (level)
  no operation moved by 1% of the time
where the time goes in v5:
time: 32.6 us; the launch traced here: 32.3 us
  Pallas kernels  13.1 us (40%)
  starting transfers between devices  9.56 us (29%)
  waiting for transfers between devices  8.07 us (25%)
  other arithmetic  0.83 us (3%)
  between operations  0.72 us (2%)
    pallas_call x1, Pallas kernels, shards(): pl.pallas_call(near_kernel, out_shape=(jax.ShapeDtypeStruct((leaves, rows...  5.51 us
    all_to_all x1, waiting for transfers between devices, shards(): lax.all_to_all(chunks, 'sub', split_axis=0, concat_axis=0, tiled=True)  5.3 us
    pallas_call x1, Pallas kernels, shards(): pl.pallas_call(final_kernel, out_shape=jax.ShapeDtypeStruct((leaves, rows...  4.27 us
    all_to_all x1, starting transfers between devices, shards(): lax.all_to_all(chunks, 'sub', split_axis=0, concat_axis=0, tiled=True)  3.47 us
    ppermute x1, starting transfers between devices, shards(): other = lax.ppermute(to_turn, 'iface', turn + [(j, i) for i, j in turn])  3.1 us
    pallas_call x1, Pallas kernels, shards(): pl.pallas_call(pack_kernel, out_shape=(toward, toward, jax.ShapeDtypeStru...  2.15 us
    ppermute x1, waiting for transfers between devices, shards(): first = lax.ppermute(to_pair, 'sub', flips(1))  1.79 us
    ppermute x1, starting transfers between devices, shards(): first = lax.ppermute(to_pair, 'sub', flips(1))  1.28 us
  transfers between devices with their start and end apart: 5, of which 3 were waited for; matrix products, arithmetic and copies ran while one was open for 3% of the time, Pallas kernels for 24%

profile of v5, /device:TPU:9, one launch (start us, length us, event | category | flops | bytes accessed | tf_op | source)
XLA Modules:
  0.0 32.3 jit_solution(1366708868169930408)
XLA Ops:
  0.0 1.2 %edges.1 = (bf16[3,256,256]{2,1,0:T(8,128)(2,1)S(1)}, bf16[3,256,256]{2,1,0:T(8,128)(2,1)S(1)}) custom-call(s32[1]{0:T(128)} %bitcast.place_hbm, s32[1,8]{1,0:T(1,128)} %count_hbm.7, bf16[1,8,256,256]{3,2,1,0:T(8,128)(2,1)} %x_hbm.5), custom_call_target="tpu_custom_call" | custom-call | flops 1 | bytes 1 | tf_op jit(solution)/shard_map/edges/pallas_call | solution.py:397
  1.2 1.3 %collective-permute-start.2 = (bf16[3,256,256]{2,1,0:T(8,128)(2,1)S(1)}, bf16[3,256,256]{2,1,0:T(8,128)(2,1)S(1)}, u32[]{:S(2)}, u32[]{:S(2)}) collective-permute-start(bf16[3,256,256]{2,1,0:T(8,128)(2,1)S(1)} %get-tuple-element.15.after_hbm), channel_id=1, source_target_pairs={{0,1},{1,0},{2,3},{3,2},{4,5},{5,4},{6,7},{7,6},{8,9},{9,8},{10,11... | collective-permute-start | bytes 1179656 | tf_op jit(solution)/shard_map/ppermute | solution.py:435
  2.5 2.1 %pack.1 = (bf16[4,64,256]{2,1,0:T(8,128)(2,1)S(1)}, bf16[4,64,256]{2,1,0:T(8,128)(2,1)S(1)}, bf16[128,256]{1,0:T(8,128)(2,1)S(1)}) custom-call(bf16[3,256,256]{2,1,0:T(8,128)(2,1)S(1)} %get-tuple-element.15.after_hbm, s32[1]{0:T(128)} %bitcast.place_hbm, s32[1,8]{1,0:T(1,128)} %count_hbm.7, s32[1,1,2,4,16]{4,3,2,1,0:T(4,128)} %send_hbm.1, ...), custom_call_target="tpu_custom_call" | custom-call | flops 1 | bytes 1 | tf_op jit(solution)/shard_map/pack/pallas_call | solution.py:412
  4.7 1.0 %collective-permute-start = (bf16[4,64,256]{2,1,0:T(8,128)(2,1)S(1)}, bf16[4,64,256]{2,1,0:T(8,128)(2,1)S(1)}, u32[]{:S(2)}, u32[]{:S(2)}) collective-permute-start(bf16[4,64,256]{2,1,0:T(8,128)(2,1)S(1)} %get-tuple-element.16), channel_id=1, source_target_pairs={{0,4},{4,0},{8,12},{12,8},{16,20},{20,16},{24,28},{28,24},{1,5},{5... | collective-permute-start | bytes 393224 | tf_op jit(solution)/shard_map/ppermute | solution.py:437
  5.7 3.1 %collective-permute-start.1 = (bf16[4,64,256]{2,1,0:T(8,128)(2,1)S(1)}, bf16[4,64,256]{2,1,0:T(8,128)(2,1)S(1)}, u32[]{:S(2)}, u32[]{:S(2)}) collective-permute-start(bf16[4,64,256]{2,1,0:T(8,128)(2,1)S(1)} %get-tuple-element.17), channel_id=1, source_target_pairs={{4,8},{12,16},{20,24},{8,4},{16,12},{24,20},{5,9},{13,17},{21,25},... | collective-permute-start | bytes 393224 | tf_op jit(solution)/shard_map/ppermute | solution.py:439
  8.8 0.7 %collective-permute-start.3 = (bf16[3,256,256]{2,1,0:T(8,128)(2,1)S(1)}, bf16[3,256,256]{2,1,0:T(8,128)(2,1)S(1)}, u32[]{:S(2)}, u32[]{:S(2)}) collective-permute-start(bf16[3,256,256]{2,1,0:T(8,128)(2,1)S(1)} %get-tuple-element.24), channel_id=1, source_target_pairs={{1,2},{2,1},{5,6},{6,5},{9,10},{10,9},{13,14},{14,13},{17,18},{18,... | collective-permute-start | bytes 1179656 | tf_op jit(solution)/shard_map/ppermute | solution.py:441
  9.5 1.8 %collective-permute-done.2.first_hbm = bf16[3,256,256]{2,1,0:T(8,128)(2,1)S(1)} collective-permute-done((bf16[3,256,256]{2,1,0:T(8,128)(2,1)S(1)}, bf16[3,256,256]{2,1,0:T(8,128)(2,1)S(1)}, u32[]{:S(2)}, u32[]{:S(2)}) %collective-permute-start.2) | collective-permute-done | bytes 393248 | tf_op jit(solution)/shard_map/ppermute | solution.py:435
  11.3 0.0 copy-start
  11.3 0.0 collective-permute-done
  11.3 1.0 %collective-permute-done.1 = bf16[4,64,256]{2,1,0:T(8,128)(2,1)S(1)} collective-permute-done((bf16[4,64,256]{2,1,0:T(8,128)(2,1)S(1)}, bf16[4,64,256]{2,1,0:T(8,128)(2,1)S(1)}, u32[]{:S(2)}, u32[]{:S(2)}) %collective-permute-start.1) | collective-permute-done | bytes 131104 | tf_op jit(solution)/shard_map/ppermute | solution.py:439
  12.3 0.0 copy-done
  12.3 0.8 %pad_maximum_fusion = bf16[4,256,256]{2,1,0:T(8,128)(2,1)} fusion(bf16[4,128,256]{2,1,0:T(8,128)(2,1)S(1)} %broadcast_in_dim.6, bf16[4,64,256]{2,1,0:T(8,128)(2,1)S(1)} %collective-permute-done.1, bf16[4,64,256]{2,1,0:T(8,128)(2,1)S(1)} %collective-permute-done), kind=kLoop, calls=%fused_computation | loop fusion | flops 1572864 | bytes 1048576 | tf_op jit(solution)/shard_map/concatenate | solution.py:444
  13.1 3.5 %all-to-all-start = ((bf16[4,256,256]{2,1,0:T(8,128)(2,1)}), bf16[4,256,256]{2,1,0:T(8,128)(2,1)S(1)}, u32[]{:S(2)}, u32[]{:S(2)}) async-start(bf16[4,256,256]{2,1,0:T(8,128)(2,1)} %pad_maximum_fusion), calls=%async_computation | async-start | bytes 1048576 | tf_op jit(solution)/shard_map/all_to_all | solution.py:445
  17.2 5.5 %near.1 = (f32[8,256,256]{2,1,0:T(8,128)S(1)}, f32[8,128]{1,0:T(8,128)S(1)}) custom-call(s32[1]{0:T(128)} %bitcast.place_hbm, s32[1,8]{1,0:T(1,128)} %count_hbm.7, s32[7,1,8]{2,1,0:T(1,128)} %bitcast.3, s32[1,8]{1,0:T(1,128)} %live_hbm.3, s32[1,1,2,4,16]{4,3,2,1,0:T(4,128)} %recv_hbm.1, s32[1,1,2,4]{3,2,1,0:T(2,128)} %recv_count_hbm.1, ...), custom_call_target="tpu_custom_call" | custom-call | flops 1 | bytes 1 | tf_op jit(solution)/shard_map/near/pallas_call | solution.py:448
  22.8 0.0 collective-permute-done.3.direct_ref
  22.8 5.3 %all-to-all-done.owned_ref = bf16[4,256,256]{2,1,0:T(8,128)(2,1)S(1)} async-done(((bf16[4,256,256]{2,1,0:T(8,128)(2,1)}), bf16[4,256,256]{2,1,0:T(8,128)(2,1)S(1)}, u32[]{:S(2)}, u32[]{:S(2)}) %all-to-all-start) | async-done | bytes 524320 | tf_op jit(solution)/shard_map/all_to_all | solution.py:445
  28.1 4.3 %final.1 = bf16[8,256,256]{2,1,0:T(8,128)(2,1)} custom-call(s32[1]{0:T(128)} %bitcast.place_hbm, s32[1,8]{1,0:T(1,128)} %count_hbm.7, s32[7,1,8]{2,1,0:T(1,128)} %bitcast.4, s32[1,8]{1,0:T(1,128)} %live_hbm.3, s32[1,1,3]{2,1,0:T(1,128)} %m2l_hbm.1, s32[1,1]{1,0:T(1,128)S(6)} %copy.15.m2l_count_hbm, bf16[1,8,7,256,256]{4,3,2,1,0:T(8,128)(2,1)} %near_hbm.3, ...), custom_call_target="tpu_custom_call" | custom-call | flops 1 | bytes 1 | tf_op jit(solution)/shard_map/final/pallas_call | solution.py:485
  (1 shorter events, 0.0 us)
Async XLA Ops:
  1.2 10.0 %collective-permute-start.2 = (bf16[3,256,256]{2,1,0:T(8,128)(2,1)S(1)}, bf16[3,256,256]{2,1,0:T(8,128)(2,1)S(1)}, u32[]{:S(2)}, u32[]{:S(2)}) collective-permute-start(bf16[3,256,256]{2,1,0:T(8,128)(2,1)S(1)} %get-tuple-element.15.after_hbm), channel_id=1, source_target_pairs={{0,1},{1,0},{2,3},{3,2},{4,5},{5,4},{6,7},{7,6},{8,9},{9,8},{10,11... | collective-permute-start | bytes 1179656 | tf_op jit(solution)/shard_map/ppermute | solution.py:435
  4.7 6.6 %collective-permute-start = (bf16[4,64,256]{2,1,0:T(8,128)(2,1)S(1)}, bf16[4,64,256]{2,1,0:T(8,128)(2,1)S(1)}, u32[]{:S(2)}, u32[]{:S(2)}) collective-permute-start(bf16[4,64,256]{2,1,0:T(8,128)(2,1)S(1)} %get-tuple-element.16), channel_id=1, source_target_pairs={{0,4},{4,0},{8,12},{12,8},{16,20},{20,16},{24,28},{28,24},{1,5},{5... | collective-permute-start | bytes 393224 | tf_op jit(solution)/shard_map/ppermute | solution.py:437
  5.7 6.6 %collective-permute-start.1 = (bf16[4,64,256]{2,1,0:T(8,128)(2,1)S(1)}, bf16[4,64,256]{2,1,0:T(8,128)(2,1)S(1)}, u32[]{:S(2)}, u32[]{:S(2)}) collective-permute-start(bf16[4,64,256]{2,1,0:T(8,128)(2,1)S(1)} %get-tuple-element.17), channel_id=1, source_target_pairs={{4,8},{12,16},{20,24},{8,4},{16,12},{24,20},{5,9},{13,17},{21,25},... | collective-permute-start | bytes 393224 | tf_op jit(solution)/shard_map/ppermute | solution.py:439
  8.8 14.0 %collective-permute-start.3 = (bf16[3,256,256]{2,1,0:T(8,128)(2,1)S(1)}, bf16[3,256,256]{2,1,0:T(8,128)(2,1)S(1)}, u32[]{:S(2)}, u32[]{:S(2)}) collective-permute-start(bf16[3,256,256]{2,1,0:T(8,128)(2,1)S(1)} %get-tuple-element.24), channel_id=1, source_target_pairs={{1,2},{2,1},{5,6},{6,5},{9,10},{10,9},{13,14},{14,13},{17,18},{18,... | collective-permute-start | bytes 1179656 | tf_op jit(solution)/shard_map/ppermute | solution.py:441
  11.3 1.0 %copy-start = (bf16[3,256,256]{2,1,0:T(8,128)(2,1)}, bf16[3,256,256]{2,1,0:T(8,128)(2,1)S(1)}, u32[]{:S(2)}) copy-start(bf16[3,256,256]{2,1,0:T(8,128)(2,1)S(1)} %collective-permute-done.2.first_hbm) | copy-start | bytes 1179652
  13.1 15.0 %all-to-all-start = ((bf16[4,256,256]{2,1,0:T(8,128)(2,1)}), bf16[4,256,256]{2,1,0:T(8,128)(2,1)S(1)}, u32[]{:S(2)}, u32[]{:S(2)}) async-start(bf16[4,256,256]{2,1,0:T(8,128)(2,1)} %pad_maximum_fusion), calls=%async_computation | async-start | bytes 1048576 | tf_op jit(solution)/shard_map/all_to_all | solution.py:445

commit v6 on v5

--- a/solution.py
+++ b/solution.py
@@ -115,10 +115,12 @@
     send = column(send).astype(INT)
     total = sides * boxes * slots
     element = lax.broadcasted_iota(INT, (total, leaves * leaf_size), 1)
-    pick = jnp.where(element == send, 1.0, 0.0).astype(BF16)
+    at = lax.broadcasted_iota(INT, (1, leaves * leaf_size), 1)
+    end = jnp.zeros_like(at)
+    for l in range(leaves):
+        end = jnp.where(at >= l * leaf_size, l * leaf_size + count_ref[0, l], end)
+    pick = jnp.where((element == send) & (at < end), 1.0, 0.0).astype(BF16)
     copies[3].wait()
-    for l in range(leaves):
-        x_ref[l] = masked_leaf(x_ref[l], count_ref[0, l])
     for c in range(4):
         comp = x_ref[:, c * leaf_size : (c + 1) * leaf_size, :]
         got = dot(pick, comp.reshape(leaves * leaf_size, fields)).astype(BF16)
@@ -126,6 +128,8 @@
             for o in range(boxes):
                 at = (s * boxes + o) * slots
                 ref[o, c * slots : (c + 1) * slots, :] = got[at : at + slots]
+    for l in range(leaves):
+        x_ref[l] = masked_leaf(x_ref[l], count_ref[0, l])
     copies[4].wait()
     blocks = jnp.concatenate([source_ref[l] for l in range(leaves)], axis=1)
     moment = dot(blocks, x_ref[...].reshape(leaves * rows, fields)).astype(BF16)

time: 32.6 us -> 32.6 us (level)
  no operation moved by 1% of the time
where the time goes in v6:
time: 32.6 us; the launch traced here: 32.3 us
  Pallas kernels  13.2 us (40%)
  starting transfers between devices  9.56 us (29%)
  waiting for transfers between devices  8.05 us (25%)
  other arithmetic  0.83 us (3%)
  between operations  0.72 us (2%)
    pallas_call x1, Pallas kernels, shards(): pl.pallas_call(near_kernel, out_shape=(jax.ShapeDtypeStruct((leaves, rows...  5.53 us
    all_to_all x1, waiting for transfers between devices, shards(): lax.all_to_all(chunks, 'sub', split_axis=0, concat_axis=0, tiled=True)  5.29 us
    pallas_call x1, Pallas kernels, shards(): pl.pallas_call(final_kernel, out_shape=jax.ShapeDtypeStruct((leaves, rows...  4.27 us
    all_to_all x1, starting transfers between devices, shards(): lax.all_to_all(chunks, 'sub', split_axis=0, concat_axis=0, tiled=True)  3.47 us
    ppermute x1, starting transfers between devices, shards(): other = lax.ppermute(to_turn, 'iface', turn + [(j, i) for i, j in turn])  3.1 us
    pallas_call x1, Pallas kernels, shards(): pl.pallas_call(pack_kernel, out_shape=(toward, toward, jax.ShapeDtypeStru...  2.15 us
    ppermute x1, waiting for transfers between devices, shards(): first = lax.ppermute(to_pair, 'sub', flips(1))  1.79 us
    ppermute x1, starting transfers between devices, shards(): first = lax.ppermute(to_pair, 'sub', flips(1))  1.28 us
  transfers between devices with their start and end apart: 5, of which 3 were waited for; matrix products, arithmetic and copies ran while one was open for 3% of the time, Pallas kernels for 24%

profile of v6, /device:TPU:9, one launch (start us, length us, event | category | flops | bytes accessed | tf_op | source)
XLA Modules:
  0.0 32.3 jit_solution(13558956721630922710)
XLA Ops:
  0.0 1.2 %edges.1 = (bf16[3,256,256]{2,1,0:T(8,128)(2,1)S(1)}, bf16[3,256,256]{2,1,0:T(8,128)(2,1)S(1)}) custom-call(s32[1]{0:T(128)} %bitcast.place_hbm, s32[1,8]{1,0:T(1,128)} %count_hbm.7, bf16[1,8,256,256]{3,2,1,0:T(8,128)(2,1)} %x_hbm.5), custom_call_target="tpu_custom_call" | custom-call | flops 1 | bytes 1 | tf_op jit(solution)/shard_map/edges/pallas_call | solution.py:401
  1.2 1.3 %collective-permute-start.2 = (bf16[3,256,256]{2,1,0:T(8,128)(2,1)S(1)}, bf16[3,256,256]{2,1,0:T(8,128)(2,1)S(1)}, u32[]{:S(2)}, u32[]{:S(2)}) collective-permute-start(bf16[3,256,256]{2,1,0:T(8,128)(2,1)S(1)} %get-tuple-element.15.after_hbm), channel_id=1, source_target_pairs={{0,1},{1,0},{2,3},{3,2},{4,5},{5,4},{6,7},{7,6},{8,9},{9,8},{10,11... | collective-permute-start | bytes 1179656 | tf_op jit(solution)/shard_map/ppermute | solution.py:439
  2.5 2.1 %pack.1 = (bf16[4,64,256]{2,1,0:T(8,128)(2,1)S(1)}, bf16[4,64,256]{2,1,0:T(8,128)(2,1)S(1)}, bf16[128,256]{1,0:T(8,128)(2,1)S(1)}) custom-call(bf16[3,256,256]{2,1,0:T(8,128)(2,1)S(1)} %get-tuple-element.15.after_hbm, s32[1]{0:T(128)} %bitcast.place_hbm, s32[1,8]{1,0:T(1,128)} %count_hbm.7, s32[1,1,2,4,16]{4,3,2,1,0:T(4,128)} %send_hbm.1, ...), custom_call_target="tpu_custom_call" | custom-call | flops 1 | bytes 1 | tf_op jit(solution)/shard_map/pack/pallas_call | solution.py:416
  4.7 1.0 %collective-permute-start = (bf16[4,64,256]{2,1,0:T(8,128)(2,1)S(1)}, bf16[4,64,256]{2,1,0:T(8,128)(2,1)S(1)}, u32[]{:S(2)}, u32[]{:S(2)}) collective-permute-start(bf16[4,64,256]{2,1,0:T(8,128)(2,1)S(1)} %get-tuple-element.16), channel_id=1, source_target_pairs={{0,4},{4,0},{8,12},{12,8},{16,20},{20,16},{24,28},{28,24},{1,5},{5... | collective-permute-start | bytes 393224 | tf_op jit(solution)/shard_map/ppermute | solution.py:441
  5.7 3.1 %collective-permute-start.1 = (bf16[4,64,256]{2,1,0:T(8,128)(2,1)S(1)}, bf16[4,64,256]{2,1,0:T(8,128)(2,1)S(1)}, u32[]{:S(2)}, u32[]{:S(2)}) collective-permute-start(bf16[4,64,256]{2,1,0:T(8,128)(2,1)S(1)} %get-tuple-element.17), channel_id=1, source_target_pairs={{4,8},{12,16},{20,24},{8,4},{16,12},{24,20},{5,9},{13,17},{21,25},... | collective-permute-start | bytes 393224 | tf_op jit(solution)/shard_map/ppermute | solution.py:443
  8.8 0.7 %collective-permute-start.3 = (bf16[3,256,256]{2,1,0:T(8,128)(2,1)S(1)}, bf16[3,256,256]{2,1,0:T(8,128)(2,1)S(1)}, u32[]{:S(2)}, u32[]{:S(2)}) collective-permute-start(bf16[3,256,256]{2,1,0:T(8,128)(2,1)S(1)} %get-tuple-element.24), channel_id=1, source_target_pairs={{1,2},{2,1},{5,6},{6,5},{9,10},{10,9},{13,14},{14,13},{17,18},{18,... | collective-permute-start | bytes 1179656 | tf_op jit(solution)/shard_map/ppermute | solution.py:445
  9.5 1.8 %collective-permute-done.2.first_hbm = bf16[3,256,256]{2,1,0:T(8,128)(2,1)S(1)} collective-permute-done((bf16[3,256,256]{2,1,0:T(8,128)(2,1)S(1)}, bf16[3,256,256]{2,1,0:T(8,128)(2,1)S(1)}, u32[]{:S(2)}, u32[]{:S(2)}) %collective-permute-start.2) | collective-permute-done | bytes 393248 | tf_op jit(solution)/shard_map/ppermute | solution.py:439
  11.3 0.0 copy-start
  11.3 0.0 collective-permute-done
  11.3 1.0 %collective-permute-done.1 = bf16[4,64,256]{2,1,0:T(8,128)(2,1)S(1)} collective-permute-done((bf16[4,64,256]{2,1,0:T(8,128)(2,1)S(1)}, bf16[4,64,256]{2,1,0:T(8,128)(2,1)S(1)}, u32[]{:S(2)}, u32[]{:S(2)}) %collective-permute-start.1) | collective-permute-done | bytes 131104 | tf_op jit(solution)/shard_map/ppermute | solution.py:443
  12.3 0.0 copy-done
  12.3 0.8 %pad_maximum_fusion = bf16[4,256,256]{2,1,0:T(8,128)(2,1)} fusion(bf16[4,128,256]{2,1,0:T(8,128)(2,1)S(1)} %broadcast_in_dim.6, bf16[4,64,256]{2,1,0:T(8,128)(2,1)S(1)} %collective-permute-done.1, bf16[4,64,256]{2,1,0:T(8,128)(2,1)S(1)} %collective-permute-done), kind=kLoop, calls=%fused_computation | loop fusion | flops 1572864 | bytes 1048576 | tf_op jit(solution)/shard_map/concatenate | solution.py:448
  13.1 3.5 %all-to-all-start = ((bf16[4,256,256]{2,1,0:T(8,128)(2,1)}), bf16[4,256,256]{2,1,0:T(8,128)(2,1)S(1)}, u32[]{:S(2)}, u32[]{:S(2)}) async-start(bf16[4,256,256]{2,1,0:T(8,128)(2,1)} %pad_maximum_fusion), calls=%async_computation | async-start | bytes 1048576 | tf_op jit(solution)/shard_map/all_to_all | solution.py:449
  17.2 5.5 %near.1 = (f32[8,256,256]{2,1,0:T(8,128)S(1)}, f32[8,128]{1,0:T(8,128)S(1)}) custom-call(s32[1]{0:T(128)} %bitcast.place_hbm, s32[1,8]{1,0:T(1,128)} %count_hbm.7, s32[7,1,8]{2,1,0:T(1,128)} %bitcast.3, s32[1,8]{1,0:T(1,128)} %live_hbm.3, s32[1,1,2,4,16]{4,3,2,1,0:T(4,128)} %recv_hbm.1, s32[1,1,2,4]{3,2,1,0:T(2,128)} %recv_count_hbm.1, ...), custom_call_target="tpu_custom_call" | custom-call | flops 1 | bytes 1 | tf_op jit(solution)/shard_map/near/pallas_call | solution.py:452
  22.8 0.0 collective-permute-done.3.direct_ref
  22.8 5.3 %all-to-all-done.owned_ref = bf16[4,256,256]{2,1,0:T(8,128)(2,1)S(1)} async-done(((bf16[4,256,256]{2,1,0:T(8,128)(2,1)}), bf16[4,256,256]{2,1,0:T(8,128)(2,1)S(1)}, u32[]{:S(2)}, u32[]{:S(2)}) %all-to-all-start) | async-done | bytes 524320 | tf_op jit(solution)/shard_map/all_to_all | solution.py:449
  28.1 4.3 %final.1 = bf16[8,256,256]{2,1,0:T(8,128)(2,1)} custom-call(s32[1]{0:T(128)} %bitcast.place_hbm, s32[1,8]{1,0:T(1,128)} %count_hbm.7, s32[7,1,8]{2,1,0:T(1,128)} %bitcast.4, s32[1,8]{1,0:T(1,128)} %live_hbm.3, s32[1,1,3]{2,1,0:T(1,128)} %m2l_hbm.1, s32[1,1]{1,0:T(1,128)S(6)} %copy.15.m2l_count_hbm, bf16[1,8,7,256,256]{4,3,2,1,0:T(8,128)(2,1)} %near_hbm.3, ...), custom_call_target="tpu_custom_call" | custom-call | flops 1 | bytes 1 | tf_op jit(solution)/shard_map/final/pallas_call | solution.py:489
  (1 shorter events, 0.0 us)
Async XLA Ops:
  1.2 10.0 %collective-permute-start.2 = (bf16[3,256,256]{2,1,0:T(8,128)(2,1)S(1)}, bf16[3,256,256]{2,1,0:T(8,128)(2,1)S(1)}, u32[]{:S(2)}, u32[]{:S(2)}) collective-permute-start(bf16[3,256,256]{2,1,0:T(8,128)(2,1)S(1)} %get-tuple-element.15.after_hbm), channel_id=1, source_target_pairs={{0,1},{1,0},{2,3},{3,2},{4,5},{5,4},{6,7},{7,6},{8,9},{9,8},{10,11... | collective-permute-start | bytes 1179656 | tf_op jit(solution)/shard_map/ppermute | solution.py:439
  4.7 6.6 %collective-permute-start = (bf16[4,64,256]{2,1,0:T(8,128)(2,1)S(1)}, bf16[4,64,256]{2,1,0:T(8,128)(2,1)S(1)}, u32[]{:S(2)}, u32[]{:S(2)}) collective-permute-start(bf16[4,64,256]{2,1,0:T(8,128)(2,1)S(1)} %get-tuple-element.16), channel_id=1, source_target_pairs={{0,4},{4,0},{8,12},{12,8},{16,20},{20,16},{24,28},{28,24},{1,5},{5... | collective-permute-start | bytes 393224 | tf_op jit(solution)/shard_map/ppermute | solution.py:441
  5.7 6.6 %collective-permute-start.1 = (bf16[4,64,256]{2,1,0:T(8,128)(2,1)S(1)}, bf16[4,64,256]{2,1,0:T(8,128)(2,1)S(1)}, u32[]{:S(2)}, u32[]{:S(2)}) collective-permute-start(bf16[4,64,256]{2,1,0:T(8,128)(2,1)S(1)} %get-tuple-element.17), channel_id=1, source_target_pairs={{4,8},{12,16},{20,24},{8,4},{16,12},{24,20},{5,9},{13,17},{21,25},... | collective-permute-start | bytes 393224 | tf_op jit(solution)/shard_map/ppermute | solution.py:443
  8.8 14.0 %collective-permute-start.3 = (bf16[3,256,256]{2,1,0:T(8,128)(2,1)S(1)}, bf16[3,256,256]{2,1,0:T(8,128)(2,1)S(1)}, u32[]{:S(2)}, u32[]{:S(2)}) collective-permute-start(bf16[3,256,256]{2,1,0:T(8,128)(2,1)S(1)} %get-tuple-element.24), channel_id=1, source_target_pairs={{1,2},{2,1},{5,6},{6,5},{9,10},{10,9},{13,14},{14,13},{17,18},{18,... | collective-permute-start | bytes 1179656 | tf_op jit(solution)/shard_map/ppermute | solution.py:445
  11.3 1.0 %copy-start = (bf16[3,256,256]{2,1,0:T(8,128)(2,1)}, bf16[3,256,256]{2,1,0:T(8,128)(2,1)S(1)}, u32[]{:S(2)}) copy-start(bf16[3,256,256]{2,1,0:T(8,128)(2,1)S(1)} %collective-permute-done.2.first_hbm) | copy-start | bytes 1179652
  13.1 15.0 %all-to-all-start = ((bf16[4,256,256]{2,1,0:T(8,128)(2,1)}), bf16[4,256,256]{2,1,0:T(8,128)(2,1)S(1)}, u32[]{:S(2)}, u32[]{:S(2)}) async-start(bf16[4,256,256]{2,1,0:T(8,128)(2,1)} %pad_maximum_fusion), calls=%async_computation | async-start | bytes 1048576 | tf_op jit(solution)/shard_map/all_to_all | solution.py:449
